TPU v7x, 128 devices: a whole 4x4x4 slice. The times are simulated.
128 devices in a mesh: leaf: 4 (over y), rows: 32 (over z, x, core).
Axes of the slice: x: 4, y: 4, z: 4, core: 2. Of those that a mesh axis runs over, the one named last changes fastest.
Arguments:
- leaf_rhs: float32 [8, 16, 2048], P(None, 'leaf', 'rows'), may hold values from -6 to 6
- parent_rhs: float32 [8, 4, 4096], P(None, 'leaf', 'rows'), may hold values from -6 to 6
- root_rhs: float32 [8, 4096], P(None, ('leaf', 'rows')), may hold values from -6 to 6
- leaf_inv: bfloat16 [16, 2048, 2048], P('leaf', 'rows'), as said below
- leaf_panel: bfloat16 [16, 8192, 2048], P('leaf', 'rows'), may hold values from -0.0625 to 0.0625
- leaf_rows: int32 [16, 8192], P('leaf', 'rows'), may hold values from 0 to 8191, as said below
- leaf_height: int32 [16], P('leaf'), may hold values from 2048 to 8192
- parent_inv: bfloat16 [4, 4096, 4096], P('leaf', 'rows'), as said below
- parent_panel: bfloat16 [4, 4096, 4096], P('leaf', 'rows'), may hold values from -0.046875 to 0.046875
- parent_rows: int32 [4, 4096], P('leaf', 'rows'), may hold values from 0 to 4095, as said below
- parent_height: int32 [4], P('leaf'), may hold values from 1024 to 4096
- root_inv: bfloat16 [4096, 4096], P('rows'), as said below
Outputs:
- leaf_solution: float32 [8, 16, 2048], P(None, 'leaf', 'rows')
- parent_solution: float32 [8, 4, 4096], P(None, 'leaf', 'rows')
- root_solution: float32 [8, 4096], P(None, ('leaf', 'rows'))
Inputs may be any that keep to these rules, and one draw needn't show every extreme that they name: `leaf_rows`: each leaf's first leaf_height entries are distinct and ascending; every entry is a valid ancestor index. `parent_rows`: each parent's first parent_height entries are distinct and ascending. `leaf_inv`: A dense well conditioned matrix. `parent_inv`: A dense well conditioned matrix. `root_inv`: A dense well conditioned matrix.
All inputs are finite; a program needn't handle non-finite values.
Results may differ from a plain program's by a relative error of at most 0.009.
Values may be sent and summed in bfloat16 or wider, within the bound.
A program may use at most 64 MiB of HBM per device.

v0:
```python
import jax
import jax.numpy as jnp
from jax import lax
from jax.sharding import PartitionSpec as P


def shards(
    leaf_rhs,
    parent_rhs,
    root_rhs,
    leaf_inv,
    leaf_panel,
    leaf_rows,
    leaf_height,
    parent_inv,
    parent_panel,
    parent_rows,
    parent_height,
    root_inv,
):
    rcount = leaf_rhs.shape[0]
    group_leaves = leaf_rhs.shape[1]
    leaf_local = leaf_panel.shape[1]
    parent_width = parent_inv.shape[2]
    root_width = root_inv.shape[1]
    row_index = lax.axis_index("rows")
    parent_cols = parent_rhs.shape[2]
    root_cols = root_rhs.shape[1]
    flat_index = lax.axis_index("leaf") * lax.axis_size("rows") + row_index
    block = leaf_inv
    ly = jnp.einsum(
        "rln,lin->rli",
        lax.all_gather(leaf_rhs.astype(jnp.bfloat16), "rows", axis=2, tiled=True),
        block,
        preferred_element_type=jnp.float32,
    )
    lyb = ly.astype(jnp.bfloat16)
    block = leaf_panel
    lupd = jnp.einsum(
        "rln,lhn->rlh",
        lax.all_gather(lyb, "rows", axis=2, tiled=True),
        block,
        preferred_element_type=jnp.float32,
    )
    leaf_pos = row_index * leaf_local + jnp.arange(leaf_local, dtype=jnp.int32)
    leaf_mask = leaf_pos[None, :] < leaf_height[:, None]
    lupd = jnp.where(leaf_mask[None, :, :], lupd, 0.0)
    leaf_flat = leaf_rows.reshape(-1)
    local_acc = (
        jnp.zeros((rcount, parent_width + root_width), jnp.float32)
        .at[:, leaf_flat]
        .add(lupd.reshape(rcount, -1))
    )
    group_acc = lax.psum(local_acc, "rows")
    parent_acc = group_acc[:, :parent_width]
    root_from_leaves = lax.psum(group_acc[:, parent_width:], "leaf")
    parent_slice = lax.dynamic_slice_in_dim(parent_acc, row_index * parent_cols, parent_cols, 1)
    prb = (parent_rhs[:, 0, :] - parent_slice).astype(jnp.bfloat16)
    inverse_rows = parent_inv[0]
    panel_rows = parent_panel[0]
    block = inverse_rows
    py = jnp.dot(
        lax.all_gather(prb, "rows", axis=1, tiled=True), block.T, preferred_element_type=jnp.float32
    )
    pyb = py.astype(jnp.bfloat16)
    parent_local = panel_rows.shape[0]
    block = panel_rows
    pupd = jnp.dot(
        lax.all_gather(pyb, "rows", axis=1, tiled=True), block.T, preferred_element_type=jnp.float32
    )
    parent_pos = row_index * parent_local + jnp.arange(parent_local, dtype=jnp.int32)
    parent_mask = parent_pos < parent_height[0]
    pupd = jnp.where(parent_mask[None, :], pupd, 0.0)
    parent_root = jnp.zeros((rcount, root_width), jnp.float32).at[:, parent_rows[0]].add(pupd)
    root_acc = root_from_leaves + lax.psum(parent_root, ("leaf", "rows"))
    root_slice = lax.dynamic_slice_in_dim(root_acc, flat_index * root_cols, root_cols, 1)
    rrb = (root_rhs - root_slice).astype(jnp.bfloat16)
    block = root_inv
    ry = jnp.dot(
        lax.all_gather(rrb, ("leaf", "rows"), axis=1, tiled=True),
        block.T,
        preferred_element_type=jnp.float32,
    )
    root_term = jnp.dot(ry.astype(jnp.bfloat16), root_inv, preferred_element_type=jnp.float32)
    root_full = lax.psum(root_term, "rows")
    root_solution = lax.dynamic_slice_in_dim(root_full, flat_index * root_cols, root_cols, 1)
    rxb = root_full.astype(jnp.bfloat16)
    parent_anc = rxb[:, parent_rows[0]]
    parent_anc = jnp.where(parent_mask[None, :], parent_anc, jnp.zeros_like(parent_anc))
    parent_term = jnp.dot(parent_anc, panel_rows, preferred_element_type=jnp.float32)
    parent_tail = lax.psum_scatter(parent_term, "rows", scatter_dimension=1, tiled=True)
    pvb = (py - parent_tail).astype(jnp.bfloat16)
    parent_sol_term = jnp.dot(pvb, inverse_rows, preferred_element_type=jnp.float32)
    parent_sol = lax.psum_scatter(parent_sol_term, "rows", scatter_dimension=1, tiled=True)
    parent_whole = lax.all_gather(parent_sol.astype(jnp.bfloat16), "rows", axis=1, tiled=True)
    ancestors = jnp.concatenate([parent_whole, rxb], axis=1)
    leaf_anc = ancestors[:, leaf_flat].reshape(rcount, group_leaves, leaf_local)
    leaf_anc = jnp.where(leaf_mask[None, :, :], leaf_anc, jnp.zeros_like(leaf_anc))
    leaf_term = jnp.einsum("rlh,lhc->rlc", leaf_anc, leaf_panel, preferred_element_type=jnp.float32)
    leaf_tail = lax.psum_scatter(leaf_term, "rows", scatter_dimension=2, tiled=True)
    lvb = (ly - leaf_tail).astype(jnp.bfloat16)
    leaf_sol_term = jnp.einsum("rli,lic->rlc", lvb, leaf_inv, preferred_element_type=jnp.float32)
    leaf_sol = lax.psum_scatter(leaf_sol_term, "rows", scatter_dimension=2, tiled=True)
    return (leaf_sol, parent_sol[:, None, :], root_solution)


def solution(mesh):
    return jax.shard_map(
        shards,
        mesh=mesh,
        in_specs=(
            P(None, "leaf", "rows"),
            P(None, "leaf", "rows"),
            P(None, ("leaf", "rows")),
            P("leaf", "rows", None),
            P("leaf", "rows", None),
            P("leaf", "rows"),
            P("leaf"),
            P("leaf", "rows", None),
            P("leaf", "rows", None),
            P("leaf", "rows"),
            P("leaf"),
            P("rows", None),
        ),
        out_specs=(P(None, "leaf", "rows"), P(None, "leaf", "rows"), P(None, ("leaf", "rows"))),
        check_vma=False,
    )
```

profile of v0, /device:TPU:1, one launch (start us, length us, event | category | flops | bytes accessed | tf_op | source)
XLA Modules:
  0.0 914.9 jit_solution(10626270217796478974)
XLA Ops:
  7.2 0.0 all-reduce.5.cloned.1.call-start
  7.2 0.8 copy.81
  8.0 0.7 copy.91
  8.7 0.1 copy.62
  8.9 28.7 %all_gather.18 = bf16[8,4,2048]{0,1,2:T(4,128)(2,1)S(1)} all-gather(bf16[8,4,64]{0,1,2:T(4,128)(2,1)S(1)} %copy.62), channel_id=1, replica_groups=mesh['leaf'=4,'rows'=32] {'rows'}, dimensions={2}, use_global_device_ids=true | all-gather | bytes 135168 | tf_op jit(solution)/shard_map/all_gather | solution.py:33
  37.6 0.8 fusion.36
  38.4 0.1 copy.64
  38.5 25.3 %all_gather.19 = bf16[8,4,2048]{0,1,2:T(4,128)(2,1)S(1)} all-gather(bf16[8,4,64]{0,1,2:T(4,128)(2,1)S(1)} %copy.64), channel_id=1, replica_groups=mesh['leaf'=4,'rows'=32] {'rows'}, dimensions={2}, use_global_device_ids=true | all-gather | bytes 135168 | tf_op jit(solution)/shard_map/all_gather | solution.py:41
  63.8 0.1 broadcast_compare_fusion
  63.9 3.4 fusion.6
  67.3 0.2 copy.66
  67.5 8.2 scatter_custom_fusion
  75.7 3.5 copy.67
  79.3 0.0 all-reduce.5.cloned.1.call-update
  79.3 0.0 all-reduce.9.cloned.1.call-start
  80.1 100.2 %all-reduce.5.cloned.1.call-done = f32[8,8192]{1,0:T(8,128)} async-done(((f32[8,8192]{1,0:T(8,128)}), f32[8,8192]{1,0:T(8,128)}) %all-reduce.5.cloned.1.call-update) | async-done | bytes 262160 | tf_op jit(solution)/shard_map/psum | solution.py:54
  180.3 1.6 fusion.35
  182.0 25.1 %all_gather.20 = bf16[8,4096]{1,0:T(8,128)(2,1)S(1)} all-gather(bf16[8,128]{1,0:T(8,128)(2,1)S(1)} %subtract_convert_fusion.3), channel_id=1, replica_groups=mesh['leaf'=4,'rows'=32] {'rows'}, dimensions={1}, use_global_device_ids=true | all-gather | bytes 67584 | tf_op jit(solution)/shard_map/all_gather | solution.py:63
  207.1 0.4 fusion.37
  207.5 21.5 %all_gather.21 = bf16[8,4096]{1,0:T(8,128)(2,1)S(1)} all-gather(bf16[8,128]{1,0:T(8,128)(2,1)S(1)} %get-tuple-element.22), channel_id=1, replica_groups=mesh['leaf'=4,'rows'=32] {'rows'}, dimensions={1}, use_global_device_ids=true | all-gather | bytes 67584 | tf_op jit(solution)/shard_map/all_gather | solution.py:69
  229.0 0.4 fusion.12
  229.4 0.1 copy.68
  229.5 1.5 scatter_custom_fusion.1
  231.0 1.2 copy.69
  232.2 0.0 all-reduce.9.cloned.1.call-update
  232.3 0.0 all-reduce.7.cloned.1.call-start
  232.3 0.7 all-reduce.7.cloned.1.call-update
  233.0 0.0 all-reduce.11.cloned.1.call-start
  233.1 140.4 %all-reduce.9.cloned.1.call-done = f32[8,4096]{1,0:T(8,128)} async-done(((f32[8,4096]{1,0:T(8,128)}), f32[8,4096]{1,0:T(8,128)}) %all-reduce.9.cloned.1.call-update) | async-done | bytes 131088 | tf_op jit(solution)/shard_map/psum | solution.py:75
  373.5 39.1 %all-reduce.7.cloned.1.call-done = f32[8,4096]{1,0:T(8,128)} async-done(((f32[8,4096]{1,0:T(8,128)}), f32[8,4096]{1,0:T(8,128)}) %all-reduce.7.cloned.1.call-update) | async-done | bytes 131088 | tf_op jit(solution)/shard_map/psum | solution.py:56
  412.6 0.8 fusion.31
  413.3 38.5 %all-gather = bf16[128,32,8]{1,2,0:T(8,128)(2,1)S(1)} all-gather(bf16[1,32,8]{1,2,0:T(8,128)(2,1)S(1)} %fusion.31), channel_id=1, replica_groups=mesh['leaf'=4,'rows'=32] {'leaf','rows'}, dimensions={0}, use_global_device_ids=true | all-gather | bytes 66048 | tf_op jit(solution)/shard_map/all_gather | solution.py:80
  451.8 0.3 reshape.142
  452.1 3.2 fusion.13
  455.3 0.0 reduce-scatter.9.cloned.1.call-start
  455.4 98.2 %all-reduce.11.cloned.1.call-done = f32[8,4096]{1,0:T(8,128)} async-done(((f32[8,4096]{1,0:T(8,128)}), f32[8,4096]{1,0:T(8,128)}) %all-reduce.11.cloned.1.call-update) | async-done | bytes 131088 | tf_op jit(solution)/shard_map/psum | solution.py:85
  553.6 0.9 convert_element_type.36
  554.5 1.3 copy.71
  555.8 2.0 gather_fusion
  557.8 1.0 fusion.14
  558.9 0.0 reduce-scatter.11.cloned.1.call-start
  558.9 69.8 %reduce-scatter.9.cloned.1.call-done = f32[8,128]{1,0:T(8,128)} async-done(((f32[8,4096]{1,0:T(8,128)}), f32[8,128]{1,0:T(8,128)}) %reduce-scatter.9.cloned.1.call-update) | async-done | bytes 4112 | tf_op jit(solution)/shard_map/reduce_scatter | solution.py:91
  628.8 1.6 fusion.17
  630.4 0.0 reduce-scatter.13.cloned.1.call-start
  630.4 73.8 %reduce-scatter.11.cloned.1.call-done = f32[8,128]{1,0:T(8,128)} async-done(((f32[8,4096]{1,0:T(8,128)}), f32[8,128]{1,0:T(8,128)}) %reduce-scatter.11.cloned.1.call-update) | async-done | bytes 4112 | tf_op jit(solution)/shard_map/reduce_scatter | solution.py:94
  704.2 0.7 convert_element_type.38
  704.9 26.1 %all_gather.23 = bf16[8,4096]{1,0:T(8,128)(2,1)S(1)} all-gather(bf16[8,128]{1,0:T(8,128)(2,1)S(1)} %convert_element_type.38), channel_id=1, replica_groups=mesh['leaf'=4,'rows'=32] {'rows'}, dimensions={1}, use_global_device_ids=true | all-gather | bytes 67584 | tf_op jit(solution)/shard_map/all_gather | solution.py:95
  731.0 1.0 copy.72
  732.0 3.2 gather_fusion.1
  735.2 0.1 copy.73
  735.3 2.8 convolution_bitcast_fusion.1
  738.2 3.1 copy.76
  741.2 4.5 reshape.143
  745.8 0.0 reduce-scatter.15.cloned.1.call-start
  745.9 74.5 %reduce-scatter.13.cloned.1.call-done = f32[64,32]{1,0:T(8,128)} async-done(((f32[2048,32]{1,0:T(8,128)}), f32[64,32]{1,0:T(8,128)}) %reduce-scatter.13.cloned.1.call-update) | async-done | bytes 8208
  820.3 0.9 reshape.144
  821.2 0.1 copy.77
  821.3 0.3 convolution_bitcast_fusion
  821.6 3.1 copy.78
  824.6 4.5 reshape.145
  829.2 1.3 constant_dynamic-slice_fusion
  830.6 75.9 %reduce-scatter.15.cloned.1.call-done = f32[64,32]{1,0:T(8,128)} async-done(((f32[2048,32]{1,0:T(8,128)}), f32[64,32]{1,0:T(8,128)}) %reduce-scatter.15.cloned.1.call-update) | async-done | bytes 8208
  906.4 0.9 reshape.146
  907.3 0.7 copy.74
  (32 shorter events, 0.2 us)
Async XLA Ops:
  7.2 30.4 %copy-start = (bf16[4,64,2048]{2,1,0:T(8,128)(2,1)S(1)}, bf16[4,64,2048]{2,1,0:T(8,128)(2,1)}, u32[]{:S(2)}) copy-start(bf16[4,64,2048]{2,1,0:T(8,128)(2,1)} %param.15) | copy-start | bytes 3145732
  7.2 173.2 %all-reduce.5.cloned.1.call-start = ((), (), s32[]{:S(2)}) async-start(), calls=%async_computation.4 | async-start | bytes 524288 | tf_op jit(solution)/shard_map/psum | solution.py:54
  37.6 26.3 %copy-start.7 = (s32[4]{0:T(128)S(1)}, s32[4]{0:T(128)}, u32[]{:S(2)}) copy-start(s32[4]{0:T(128)} %param.18) | copy-start | bytes 52
  75.7 3.6 copy-start.8
  75.7 106.2 %copy-start.5 = (f32[8,1,128]{2,1,0:T(1,128)S(1)}, f32[8,1,128]{2,1,0:T(1,128)}, u32[]{:S(2)}) copy-start(f32[8,1,128]{2,1,0:T(1,128)} %param.13) | copy-start | bytes 12292
  75.7 131.4 %copy-start.3 = (bf16[1,128,4096]{2,1,0:T(8,128)(2,1)S(1)}, bf16[1,128,4096]{2,1,0:T(8,128)(2,1)}, u32[]{:S(2)}) copy-start(bf16[1,128,4096]{2,1,0:T(8,128)(2,1)} %param.19) | copy-start | bytes 3145732
  79.3 149.7 %copy-start.1 = (bf16[1,128,4096]{2,1,0:T(8,128)(2,1)S(1)}, bf16[1,128,4096]{2,1,0:T(8,128)(2,1)}, u32[]{:S(2)}) copy-start(bf16[1,128,4096]{2,1,0:T(8,128)(2,1)} %param.20) | copy-start | bytes 3145732
  79.3 294.2 %all-reduce.9.cloned.1.call-start = ((), (), s32[]{:S(2)}) async-start(), calls=%async_computation.6 | async-start | bytes 262144 | tf_op jit(solution)/shard_map/psum | solution.py:75
  229.5 183.1 %copy-start.6 = (f32[8,32]{1,0:T(8,128)S(1)}, f32[8,32]{1,0:T(8,128)}, u32[]{:S(2)}) copy-start(f32[8,32]{1,0:T(8,128)} %param.14) | copy-start | bytes 3076
  232.3 180.3 %all-reduce.7.cloned.1.call-start = ((), (), s32[]{:S(2)}) async-start(), calls=%async_computation.5 | async-start | bytes 262144 | tf_op jit(solution)/shard_map/psum | solution.py:56
  233.0 320.6 %all-reduce.11.cloned.1.call-start = ((), (), s32[]{:S(2)}) async-start(), calls=%async_computation.7 | async-start | bytes 262144 | tf_op jit(solution)/shard_map/psum | solution.py:85
  451.8 106.0 %copy-start.2 = (bf16[1,128,4096]{2,1,0:T(8,128)(2,1)S(1)}, bf16[1,128,4096]{2,1,0:T(8,128)(2,1)}, u32[]{:S(2)}) copy-start(bf16[1,128,4096]{2,1,0:T(8,128)(2,1)} %param.20) | copy-start | bytes 3145732
  452.1 176.6 %copy-start.4 = (bf16[1,128,4096]{2,1,0:T(8,128)(2,1)S(1)}, bf16[1,128,4096]{2,1,0:T(8,128)(2,1)}, u32[]{:S(2)}) copy-start(bf16[1,128,4096]{2,1,0:T(8,128)(2,1)} %param.19) | copy-start | bytes 3145732
  455.3 173.4 %reduce-scatter.9.cloned.1.call-start = ((), (), s32[]{:S(2)}) async-start(), calls=%async_computation.8 | async-start | bytes 135168 | tf_op jit(solution)/shard_map/reduce_scatter | solution.py:91
  558.9 145.3 %reduce-scatter.11.cloned.1.call-start = ((), (), s32[]{:S(2)}) async-start(), calls=%async_computation.9 | async-start | bytes 135168 | tf_op jit(solution)/shard_map/reduce_scatter | solution.py:94
  630.4 190.0 %reduce-scatter.13.cloned.1.call-start = ((), (), s32[]{:S(2)}) async-start(), calls=%async_computation.10 | async-start | bytes 1081344
  745.8 160.6 %reduce-scatter.15.cloned.1.call-start = ((), (), s32[]{:S(2)}) async-start(), calls=%async_computation.11 | async-start | bytes 1081344
Sparse Core Ops, SparseCore 0:
  79.4 100.8 all-reduce.4
  232.4 141.0 all-reduce.8
  375.8 36.7 all-reduce.6
  455.4 98.0 all-reduce.10
  559.0 69.7 reduce-scatter.8
  632.6 71.5 reduce-scatter.10
  745.9 74.3 reduce-scatter.12
  829.3 77.0 reduce-scatter.14
where the time goes:
time: 917 us; the launch traced here: 915 us
  waiting for transfers between devices  673 us (73%)
  blocking collectives  165 us (18%)
  local copies, waits for them, and re-layouts  35.6 us (4%)
  between operations  15.1 us (2%)
  matrix products  13.8 us (2%)
  other arithmetic  12.2 us (1%)
    unnamed x10, waiting for transfers between devices  151 us
    psum x1, waiting for transfers between devices, shards(): root_acc = root_from_leaves + lax.psum(parent_root, ('leaf', 'rows'))  140 us
    psum x1, waiting for transfers between devices, shards(): group_acc = lax.psum(local_acc, 'rows')  100 us
    psum x1, waiting for transfers between devices, shards(): root_full = lax.psum(root_term, 'rows')  98.2 us
    reduce_scatter x1, waiting for transfers between devices, shards(): lax.psum_scatter(parent_sol_term, 'rows', scatter_dimension=1, tiled=True)  73.8 us
    reduce_scatter x1, waiting for transfers between devices, shards(): lax.psum_scatter(parent_term, 'rows', scatter_dimension=1, tiled=True)  69.8 us
    psum x1, waiting for transfers between devices, shards(): root_from_leaves = lax.psum(group_acc[:, parent_width:], 'leaf')  39.1 us
    all_gather x1, blocking collectives, shards(): lax.all_gather(rrb, ('leaf', 'rows'), axis=1, tiled=True)  38.5 us
  transfers between devices with their start and end apart: 8, of which 8 were waited for; matrix products, arithmetic and copies ran while one was open for 0% of the time, Pallas kernels for 0%

commit v1 on v0

v1 whole, which is shorter than its diff:
```python
import functools

import jax
import jax.numpy as jnp
from jax import lax
from jax.experimental import pallas as pl
from jax.experimental.pallas import tpu as pltpu
from jax.sharding import PartitionSpec as P

F32 = jnp.float32
BF16 = jnp.bfloat16
LANES = 128
HALF = 64
NT = (((1,), (1,)), ((), ()))
PHASES = 15


def dot(a, b):
    return jnp.dot(a, b, preferred_element_type=F32)


def dot_nt(a, b):
    return lax.dot_general(a, b, NT, preferred_element_type=F32)


def swap_halves(x):
    return pltpu.roll(x, HALF, 1)


def kernel(
    n,
    groups,
    leaf_rhs,
    parent_rhs,
    root_rhs,
    leaf_rows,
    leaf_height,
    parent_rows,
    parent_height,
    leaf_inv_hbm,
    leaf_panel_hbm,
    parent_inv_hbm,
    parent_panel_hbm,
    root_inv_hbm,
    leaf_out,
    parent_out,
    root_out,
    leaf_inv,
    leaf_panel,
    parent_inv,
    parent_panel,
    root_inv,
    onehot,
    onehot_p,
    xs,
    spread_hi,
    spread_lo,
    terms,
    g1,
    g2,
    s3,
    r3,
    g4,
    g5,
    s6,
    r6,
    g7a,
    g7b,
    s8,
    r8,
    g9,
    s10,
    r10,
    s11,
    r11,
    g12,
    s13,
    r13,
    s14,
    r14,
    load_sem,
    send_sem,
    recv_sem,
):
    group = lax.axis_index("leaf")
    me = lax.axis_index("rows")

    barrier = pltpu.get_barrier_semaphore()

    def greet_row(i, carry):
        pl.semaphore_signal(barrier, inc=1, device_id={"rows": lax.rem(me + i, n)})
        return carry

    lax.fori_loop(1, n, greet_row, 0)
    for i in range(1, groups):
        pl.semaphore_signal(barrier, inc=1, device_id={"leaf": lax.rem(group + i, groups)})

    loads = [
        pltpu.make_async_copy(src, dst, load_sem.at[i])
        for i, (src, dst) in enumerate(
            (
                (leaf_inv_hbm, leaf_inv),
                (leaf_panel_hbm, leaf_panel),
                (parent_inv_hbm, parent_inv),
                (parent_panel_hbm, parent_panel),
                (root_inv_hbm, root_inv),
            )
        )
    ]
    for copy in loads:
        copy.start()

    low = lax.broadcasted_iota(jnp.int32, (8, LANES), 1) < HALF
    low16 = lax.broadcasted_iota(jnp.int32, (16, LANES), 1) < HALF

    def drain(ref, sem, count):
        view = ref.at[pl.ds(0, count)]
        pltpu.make_async_copy(view, view, sem).wait()

    def gather_start(ref, value, phase):
        ref[me] = value

        def send(i, carry):
            pltpu.make_async_remote_copy(
                src_ref=ref.at[me],
                dst_ref=ref.at[me],
                send_sem=send_sem.at[phase],
                recv_sem=recv_sem.at[phase],
                device_id={"rows": lax.rem(me + i, n)},
            ).start()
            return carry

        lax.fori_loop(1, n, send, 0)

    def gather_wait(ref, phase):
        drain(ref, recv_sem.at[phase], n - 1)

    def scatter_start(src, dst, phase):
        def send(i, carry):
            peer = lax.rem(me + i, n)
            pltpu.make_async_remote_copy(
                src_ref=src.at[peer],
                dst_ref=dst.at[me],
                send_sem=send_sem.at[phase],
                recv_sem=recv_sem.at[phase],
                device_id={"rows": peer},
            ).start()
            return carry

        lax.fori_loop(1, n, send, 0)
        dst[me] = src[me]

    def scatter_sum(dst, phase):
        drain(dst, recv_sem.at[phase], n - 1)
        return jnp.sum(dst[...], axis=0)

    def pack_rhs():
        tops = [
            jnp.concatenate([leaf_rhs[:, 2 * a, :], leaf_rhs[:, 2 * a + 1, :]], axis=1)
            for a in range(2)
        ]
        return jnp.concatenate(tops, axis=0).astype(BF16)

    def unpack(ref):
        for c in range(n // 2):
            even = ref[2 * c].astype(F32)
            odd = ref[2 * c + 1].astype(F32)
            cols = pl.ds(c * LANES, LANES)
            xs[0:16, cols] = jnp.where(low16, even, swap_halves(odd)).astype(BF16)
            xs[16:32, cols] = jnp.where(low16, swap_halves(even), odd).astype(BF16)

    def pack_terms(dst):
        for c in range(n // 2):
            cols = pl.ds(c * LANES, LANES)
            for a in range(2):
                rows = pl.ds(8 * a, 8)
                even = terms[pl.ds(16 * a, 8), cols]
                odd = terms[pl.ds(16 * a + 8, 8), cols]
                dst[2 * c, rows, :] = jnp.where(low, even, swap_halves(odd))
                dst[2 * c + 1, rows, :] = jnp.where(low, swap_halves(even), odd)

    def columns(ref):
        return jnp.concatenate([ref[c] for c in range(n)], axis=1)

    def spread(value, where_at, blocks, width):
        high = value.astype(BF16).astype(F32)
        rest = value - high
        for q in range(0, blocks, 2):
            rows = pl.ds(8 * q, 16)
            for part, ref in ((high, spread_hi), (rest, spread_lo)):
                pair = [jnp.where(where_at == q + k, part, 0.0) for k in range(2)]
                ref[rows, 0:width] = jnp.concatenate(pair, axis=0).astype(BF16)

    def pick(table, where_at, first):
        total = jnp.zeros(where_at.shape, F32)
        for q in range(n):
            total += jnp.where(where_at == first + q, table[8 * q : 8 * q + 8, :], 0.0)
        return total

    packed_rhs = pack_rhs()
    pl.semaphore_wait(barrier, n - 1 + groups - 1)
    gather_start(g1, packed_rhs, 0)

    piece = leaf_rows.shape[1]
    at_list, low_list = [], []
    for s in range(4):
        rows_s = leaf_rows[s : s + 1, :]
        pos = me * piece + lax.broadcasted_iota(jnp.int32, (1, piece), 1)
        at_list.append(jnp.where(pos < leaf_height[s], rows_s >> 7, -1))
        low_list.append(rows_s & (LANES - 1))
    height = 4 * piece
    leaf_at = jnp.broadcast_to(jnp.concatenate(at_list, axis=1), (8, height))
    leaf_low = jnp.concatenate(low_list, axis=1)
    onehot[...] = jnp.where(
        lax.broadcasted_iota(jnp.int32, (LANES, height), 0) == leaf_low, 1.0, 0.0
    ).astype(BF16)
    rows_p = parent_rows[...]
    pos_p = me * LANES + lax.broadcasted_iota(jnp.int32, (1, LANES), 1)
    parent_at = jnp.broadcast_to(
        jnp.where(pos_p < parent_height[0], rows_p >> 7, -1), (8, LANES)
    )
    onehot_p[...] = jnp.where(
        lax.broadcasted_iota(jnp.int32, (LANES, LANES), 0) == (rows_p & (LANES - 1)), 1.0, 0.0
    ).astype(BF16)

    loads[0].wait()
    gather_wait(g1, 0)
    unpack(g1)
    full = dot_nt(xs[...], leaf_inv[...])
    ly = jnp.concatenate(
        [
            jnp.where(low, full[0:8, 0:LANES], full[16:24, 0:LANES]),
            jnp.where(low, full[8:16, LANES:], full[24:32, LANES:]),
        ],
        axis=0,
    )
    gather_start(g2, ly.astype(BF16), 1)
    loads[1].wait()
    gather_wait(g2, 1)
    unpack(g2)
    updates = []
    for s in range(4):
        a, b = s // 2, s % 2
        got = dot_nt(xs[16 * b : 16 * b + 16, :], leaf_panel[pl.ds(s * piece, piece), :])
        updates.append(got[8 * a : 8 * a + 8, :])
    spread(jnp.concatenate(updates, axis=1), leaf_at, 2 * n, height)
    acc = dot_nt(spread_hi[...], onehot[...]) + dot_nt(spread_lo[...], onehot[...])
    for q in range(2 * n):
        s3[q % n, q // n] = acc[8 * q : 8 * q + 8, :]
    width = root_rhs.shape[1]
    per_slab = LANES // width
    slab = lax.div(group * n + me, per_slab)
    part = lax.rem(me, per_slab)
    lane_part = lax.broadcasted_iota(jnp.int32, (8, LANES), 1) // width
    mine = jnp.concatenate([root_rhs[...]] * per_slab, axis=1)
    s3[slab, 1] = s3[slab, 1] - jnp.where(lane_part == part, mine, 0.0)
    scatter_start(s3, r3, 2)
    sums = scatter_sum(r3, 2)

    prb = (parent_rhs[...] - sums[0]).astype(BF16)
    gather_start(g4, prb, 3)
    loads[2].wait()
    gather_wait(g4, 3)
    py = dot_nt(columns(g4), parent_inv[...])
    gather_start(g5, py.astype(BF16), 4)
    loads[3].wait()
    gather_wait(g5, 4)
    pupd = dot_nt(columns(g5), parent_panel[...])
    spread(pupd, parent_at, n, LANES)
    acc_p = dot_nt(spread_hi[0 : 8 * n, 0:LANES], onehot_p[...]) + dot_nt(
        spread_lo[0 : 8 * n, 0:LANES], onehot_p[...]
    )
    for q in range(n):
        s6[q] = acc_p[8 * q : 8 * q + 8, :]
    scatter_start(s6, r6, 5)
    partial = scatter_sum(r6, 5) + sums[1]

    g7a[group] = partial
    for i in range(1, groups):
        pltpu.make_async_remote_copy(
            src_ref=g7a.at[group],
            dst_ref=g7a.at[group],
            send_sem=send_sem.at[6],
            recv_sem=recv_sem.at[6],
            device_id={"leaf": lax.rem(group + i, groups)},
        ).start()
    drain(g7a, recv_sem.at[6], groups - 1)
    rrb = (-jnp.sum(g7a[...], axis=0)).astype(BF16)
    gather_start(g7b, rrb, 7)
    loads[4].wait()
    gather_wait(g7b, 7)
    ry = dot_nt(columns(g7b), root_inv[...])
    root_term = dot(ry.astype(BF16), root_inv[...])
    for c in range(n):
        s8[c] = root_term[:, c * LANES : (c + 1) * LANES]
    scatter_start(s8, r8, 8)
    root_slab = scatter_sum(r8, 8)
    gather_start(g9, root_slab.astype(BF16), 9)
    gather_wait(g9, 9)

    rxb = g9[...].reshape(n * 8, LANES)
    parent_anc = pick(dot(rxb, onehot_p[...]), parent_at, 0).astype(BF16)
    parent_term = dot(parent_anc, parent_panel[...])
    for c in range(n):
        s10[c] = parent_term[:, c * LANES : (c + 1) * LANES]
    scatter_start(s10, r10, 10)
    leaf_anc = pick(dot(rxb, onehot[...]), leaf_at, n)
    mine = jnp.where(lane_part == part, g9[slab].astype(F32), 0.0)
    root_out[...] = functools.reduce(
        lambda x, y: x + y, [mine[:, k * width : (k + 1) * width] for k in range(per_slab)]
    )
    pvb = (py - scatter_sum(r10, 10)).astype(BF16)
    parent_term = dot(pvb, parent_inv[...])
    for c in range(n):
        s11[c] = parent_term[:, c * LANES : (c + 1) * LANES]
    scatter_start(s11, r11, 11)
    parent_sol = scatter_sum(r11, 11)
    parent_out[...] = parent_sol
    gather_start(g12, parent_sol.astype(BF16), 12)
    gather_wait(g12, 12)

    pxb = g12[...].reshape(n * 8, LANES)
    leaf_anc = (leaf_anc + pick(dot(pxb, onehot[...]), leaf_at, 0)).astype(BF16)
    for s in range(4):
        terms[pl.ds(8 * s, 8), :] = dot(
            leaf_anc[:, s * piece : (s + 1) * piece], leaf_panel[pl.ds(s * piece, piece), :]
        )
    pack_terms(s13)
    scatter_start(s13, r13, 13)
    lvb = ly - scatter_sum(r13, 13)
    none = jnp.zeros((8, LANES), F32)
    blocks = []
    for s in range(4):
        a, b = s // 2, s % 2
        held = jnp.where(low if b == 0 else ~low, lvb[8 * a : 8 * a + 8, :], 0.0)
        blocks.append(jnp.concatenate([held, none] if a == 0 else [none, held], axis=1))
    terms[...] = dot(jnp.concatenate(blocks, axis=0).astype(BF16), leaf_inv[...])
    pack_terms(s14)
    scatter_start(s14, r14, 14)
    leaf_out[...] = scatter_sum(r14, 14)

    for phase, ref in enumerate(
        (g1, g2, r3, g4, g5, r6, g7a, g7b, r8, g9, r10, r11, g12, r13, r14)
    ):
        drain(ref, send_sem.at[phase], (groups if phase == 6 else n) - 1)


def solution(mesh):
    n = mesh.shape["rows"]
    groups = mesh.shape["leaf"]

    def shards(
        leaf_rhs,
        parent_rhs,
        root_rhs,
        leaf_inv,
        leaf_panel,
        leaf_rows,
        leaf_height,
        parent_inv,
        parent_panel,
        parent_rows,
        parent_height,
        root_inv,
    ):
        leaf_cols = leaf_inv.shape[2]
        cols = root_inv.shape[1]
        height = 4 * leaf_panel.shape[1]
        packed = (16, LANES)
        vmem = pl.BlockSpec(memory_space=pltpu.VMEM)
        smem = pl.BlockSpec(memory_space=pltpu.SMEM)
        hbm = pl.BlockSpec(memory_space=pl.ANY)
        slabs = (n, 8, LANES)
        buffers = [
            ((n, *packed), BF16),
            ((n, *packed), BF16),
            ((n, 2, 8, LANES), F32),
            ((n, 2, 8, LANES), F32),
            (slabs, BF16),
            (slabs, BF16),
            (slabs, F32),
            (slabs, F32),
            ((groups, 8, LANES), F32),
            (slabs, BF16),
            (slabs, F32),
            (slabs, F32),
            (slabs, BF16),
            (slabs, F32),
            (slabs, F32),
            (slabs, F32),
            (slabs, F32),
            (slabs, BF16),
            ((n, *packed), F32),
            ((n, *packed), F32),
            ((n, *packed), F32),
            ((n, *packed), F32),
        ]
        leaf_out, parent_out, root_out = pl.pallas_call(
            functools.partial(kernel, n, groups),
            out_shape=(
                jax.ShapeDtypeStruct(packed, F32),
                jax.ShapeDtypeStruct((8, LANES), F32),
                jax.ShapeDtypeStruct(root_rhs.shape, F32),
            ),
            in_specs=[vmem, vmem, vmem, vmem, smem, vmem, smem] + [hbm] * 5,
            out_specs=(vmem, vmem, vmem),
            scratch_shapes=[
                pltpu.VMEM((256, leaf_cols), BF16),
                pltpu.VMEM((height, leaf_cols), BF16),
                pltpu.VMEM((LANES, cols), BF16),
                pltpu.VMEM((LANES, cols), BF16),
                pltpu.VMEM((LANES, cols), BF16),
                pltpu.VMEM((LANES, height), BF16),
                pltpu.VMEM((LANES, LANES), BF16),
                pltpu.VMEM((32, leaf_cols), BF16),
                pltpu.VMEM((16 * n, height), BF16),
                pltpu.VMEM((16 * n, height), BF16),
                pltpu.VMEM((32, leaf_cols), F32),
            ]
            + [pltpu.VMEM(shape, kind) for shape, kind in buffers]
            + [
                pltpu.SemaphoreType.DMA((5,)),
                pltpu.SemaphoreType.DMA((PHASES,)),
                pltpu.SemaphoreType.DMA((PHASES,)),
            ],
            compiler_params=pltpu.CompilerParams(
                collective_id=0, has_side_effects=True, vmem_limit_bytes=48 << 20
            ),
            name="solve",
        )(
            leaf_rhs,
            parent_rhs[:, 0, :],
            root_rhs,
            leaf_rows,
            leaf_height,
            parent_rows,
            parent_height,
            leaf_inv.reshape(-1, leaf_cols),
            leaf_panel.reshape(-1, leaf_cols),
            parent_inv[0],
            parent_panel[0],
            root_inv,
        )
        leaf_sol = leaf_out.reshape(2, 8, 2, HALF).transpose(1, 0, 2, 3).reshape(8, 4, HALF)
        return leaf_sol, parent_out[:, None, :], root_out

    return jax.shard_map(
        shards,
        mesh=mesh,
        in_specs=(
            P(None, "leaf", "rows"),
            P(None, "leaf", "rows"),
            P(None, ("leaf", "rows")),
            P("leaf", "rows", None),
            P("leaf", "rows", None),
            P("leaf", "rows"),
            P("leaf"),
            P("leaf", "rows", None),
            P("leaf", "rows", None),
            P("leaf", "rows"),
            P("leaf"),
            P("rows", None),
        ),
        out_specs=(P(None, "leaf", "rows"), P(None, "leaf", "rows"), P(None, ("leaf", "rows"))),
        check_vma=False,
    )
```

time: 917 us -> 106 us (0.12)
  waiting for transfers between devices: 673 us -> 0 us
  blocking collectives: 165 us -> 0 us
  Pallas kernels: 0 us -> 93.1 us
  local copies, waits for them, and re-layouts: 35.6 us -> 10.9 us
  matrix products: 13.8 us -> 0 us
  between operations: 15.1 us -> 1.31 us
  other arithmetic: 12.2 us -> 0 us
    psum x4 -> x0, waiting for transfers between devices: 378 us -> none  [the longest x1 140 us: shards(): root_acc = root_from_leaves + lax.psum(parent_root, ('leaf', 'rows'))]
    all_gather x6 -> x0, blocking collectives: 165 us -> none  [the longest x1 38.5 us: shards(): lax.all_gather(rrb, ('leaf', 'rows'), axis=1, tiled=True)]
    unnamed x10 -> x0, waiting for transfers between devices: 151 us -> none
    reduce_scatter x2 -> x0, waiting for transfers between devices: 144 us -> none  [the longest x1 73.8 us: shards(): lax.psum_scatter(parent_sol_term, 'rows', scatter_dimension=1, tiled=True)]
    pallas_call x0 -> x1, Pallas kernels: none -> 93.1 us  [shards(): pl.pallas_call(functools.partial(kernel, n, groups), out_shape=(jax.Shape...]
    dot_general x9 -> x0, matrix products: 13.8 us -> none  [the longest x1 3.4 us: shards(): jnp.einsum('rln,lhn->rlh', lax.all_gather(lyb, 'rows', axis=2, tiled=True...]
    scatter-add x2 -> x0, other arithmetic: 9.7 us -> none  [the longest x1 8.19 us: shards(): local_acc = jnp.zeros((rcount, parent_width + root_width), jnp.float32).a...]
    unnamed x29 -> x22, local copies, waits for them, and re-layouts: 19.6 us -> 10.2 us
  transfers between devices with their start and end apart: 8 -> 0, of which waited for: 8 -> 0; matrix products, arithmetic and copies ran while one was open for 0% -> 0% of each run, Pallas kernels for 0% -> 0%
where the time goes in v1:
time: 106 us; the launch traced here: 105 us
  Pallas kernels  93.1 us (88%)
  local copies, waits for them, and re-layouts  10.9 us (10%)
  between operations  1.31 us (1%)
    pallas_call x1, Pallas kernels, shards(): pl.pallas_call(functools.partial(kernel, n, groups), out_shape=(jax.Shape...  93.1 us
    unnamed x22, local copies, waits for them, and re-layouts  10.2 us

profile of v1, /device:TPU:1, one launch (start us, length us, event | category | flops | bytes accessed | tf_op | source)
XLA Modules:
  0.0 105.2 jit_solution(3919843356255338190)
XLA Ops:
  1.3 0.0 copy-start
  1.3 1.2 %copy-done = bf16[4,64,2048]{2,1,0:T(8,128)(2,1)S(1)} copy-done((bf16[4,64,2048]{2,1,0:T(8,128)(2,1)S(1)}, bf16[4,64,2048]{2,1,0:T(8,128)(2,1)}, u32[]{:S(2)}) %copy-start) | copy-done | bytes 1048600
  2.5 0.0 copy-start.1
  2.5 1.2 %copy-done.1 = bf16[1,128,4096]{2,1,0:T(8,128)(2,1)S(1)} copy-done((bf16[1,128,4096]{2,1,0:T(8,128)(2,1)S(1)}, bf16[1,128,4096]{2,1,0:T(8,128)(2,1)}, u32[]{:S(2)}) %copy-start.1) | copy-done | bytes 1048600
  3.7 0.0 copy-start.2
  3.7 1.2 %copy-done.2 = bf16[1,128,4096]{2,1,0:T(8,128)(2,1)S(1)} copy-done((bf16[1,128,4096]{2,1,0:T(8,128)(2,1)S(1)}, bf16[1,128,4096]{2,1,0:T(8,128)(2,1)}, u32[]{:S(2)}) %copy-start.2) | copy-done | bytes 1048600
  5.0 0.0 copy-start.3
  5.0 1.2 %copy-done.3 = bf16[128,4096]{1,0:T(8,128)(2,1)S(1)} copy-done((bf16[128,4096]{1,0:T(8,128)(2,1)S(1)}, bf16[128,4096]{1,0:T(8,128)(2,1)}, u32[]{:S(2)}) %copy-start.3) | copy-done | bytes 1048600
  6.2 0.0 copy-start.4
  6.2 0.7 copy-done.4
  6.9 0.0 copy-start.5
  6.9 0.7 copy-done.5
  7.6 0.0 copy-start.6
  7.6 0.7 copy-done.6
  8.3 0.0 copy-start.7
  8.3 0.7 copy-done.7
  9.0 0.0 copy-start.8
  9.0 0.7 copy-done.8
  9.6 0.0 copy-start.9
  9.6 0.7 copy-done.9
  10.3 93.1 %solve.1 = (f32[16,128]{1,0:T(8,128)S(1)}, f32[8,128]{1,0:T(8,128)S(1)}, f32[8,32]{1,0:T(8,128)S(1)}) custom-call(f32[8,4,64]{2,1,0:T(4,128)S(1)} %copy-done.4, f32[8,128]{1,0:T(8,128)S(1)} %bitcast.13, f32[8,32]{1,0:T(8,128)S(1)} %copy-done.6, s32[4,256]{1,0:T(4,128)S(1)} %copy-done.7, s32[4]{0:T(128)S(1)} %copy-done.8, s32[1,128]{1,0:T(1,128)S(1)} %copy-done.9, ...), custom_call_target="tpu_custom_call" | custom-call | tf_op jit(solution)/shard_map/solve/pallas_call | solution.py:398
  103.4 0.1 reshape.20
  103.4 0.6 copy.15
  104.1 0.6 copy.20
  104.7 0.6 copy.21
Async XLA Ops:
  1.3 1.2 %copy-start = (bf16[4,64,2048]{2,1,0:T(8,128)(2,1)S(1)}, bf16[4,64,2048]{2,1,0:T(8,128)(2,1)}, u32[]{:S(2)}) copy-start(bf16[4,64,2048]{2,1,0:T(8,128)(2,1)} %param.15) | copy-start | bytes 3145732
  2.5 1.2 %copy-start.1 = (bf16[1,128,4096]{2,1,0:T(8,128)(2,1)S(1)}, bf16[1,128,4096]{2,1,0:T(8,128)(2,1)}, u32[]{:S(2)}) copy-start(bf16[1,128,4096]{2,1,0:T(8,128)(2,1)} %param.19) | copy-start | bytes 3145732
  3.7 1.2 %copy-start.2 = (bf16[1,128,4096]{2,1,0:T(8,128)(2,1)S(1)}, bf16[1,128,4096]{2,1,0:T(8,128)(2,1)}, u32[]{:S(2)}) copy-start(bf16[1,128,4096]{2,1,0:T(8,128)(2,1)} %param.20) | copy-start | bytes 3145732
  5.0 1.2 %copy-start.3 = (bf16[128,4096]{1,0:T(8,128)(2,1)S(1)}, bf16[128,4096]{1,0:T(8,128)(2,1)}, u32[]{:S(2)}) copy-start(bf16[128,4096]{1,0:T(8,128)(2,1)} %root_inv_hbm.1) | copy-start | bytes 3145732
  6.2 0.7 copy-start.4
  6.9 0.7 copy-start.5
  7.6 0.7 copy-start.6
  8.3 0.7 copy-start.7
  9.0 0.7 copy-start.8
  9.6 0.7 copy-start.9

commit v2 on v1

--- a/solution.py
+++ b/solution.py
@@ -30,13 +30,13 @@
 def kernel(
     n,
     groups,
-    leaf_rhs,
-    parent_rhs,
-    root_rhs,
-    leaf_rows,
-    leaf_height,
-    parent_rows,
-    parent_height,
+    leaf_rhs_hbm,
+    parent_rhs_hbm,
+    root_rhs_hbm,
+    leaf_rows_hbm,
+    leaf_height_hbm,
+    parent_rows_hbm,
+    parent_height_hbm,
     leaf_inv_hbm,
     leaf_panel_hbm,
     parent_inv_hbm,
@@ -45,6 +45,13 @@
     leaf_out,
     parent_out,
     root_out,
+    leaf_rhs,
+    parent_rhs,
+    root_rhs,
+    leaf_rows,
+    leaf_height,
+    parent_rows,
+    parent_height,
     leaf_inv,
     leaf_panel,
     parent_inv,
@@ -87,11 +94,23 @@
 
     barrier = pltpu.get_barrier_semaphore()
 
+    def peer_of(i):
+        if n != 32:
+            return lax.rem(me + i + 1, n)
+
+        def far_first(a):
+            high = lax.div(a, 2)
+            return 2 * (1 - high) + lax.rem(high + a, 2)
+
+        z = lax.rem(lax.div(me, 8) + far_first(lax.div(i, 8)), 4)
+        x = lax.rem(lax.div(me, 2) + far_first(lax.rem(lax.div(i, 2), 4)), 4)
+        return 8 * z + 2 * x + lax.rem(me + 1 - lax.rem(i, 2), 2)
+
     def greet_row(i, carry):
-        pl.semaphore_signal(barrier, inc=1, device_id={"rows": lax.rem(me + i, n)})
+        pl.semaphore_signal(barrier, inc=1, device_id={"rows": peer_of(i)})
         return carry
 
-    lax.fori_loop(1, n, greet_row, 0)
+    lax.fori_loop(0, n - 1, greet_row, 0)
     for i in range(1, groups):
         pl.semaphore_signal(barrier, inc=1, device_id={"leaf": lax.rem(group + i, groups)})
 
@@ -99,6 +118,13 @@
         pltpu.make_async_copy(src, dst, load_sem.at[i])
         for i, (src, dst) in enumerate(
             (
+                (leaf_rhs_hbm, leaf_rhs),
+                (leaf_rows_hbm, leaf_rows),
+                (leaf_height_hbm, leaf_height),
+                (parent_rows_hbm, parent_rows),
+                (parent_height_hbm, parent_height),
+                (root_rhs_hbm, root_rhs),
+                (parent_rhs_hbm, parent_rhs),
                 (leaf_inv_hbm, leaf_inv),
                 (leaf_panel_hbm, leaf_panel),
                 (parent_inv_hbm, parent_inv),
@@ -126,18 +152,18 @@
                 dst_ref=ref.at[me],
                 send_sem=send_sem.at[phase],
                 recv_sem=recv_sem.at[phase],
-                device_id={"rows": lax.rem(me + i, n)},
+                device_id={"rows": peer_of(i)},
             ).start()
             return carry
 
-        lax.fori_loop(1, n, send, 0)
+        lax.fori_loop(0, n - 1, send, 0)
 
     def gather_wait(ref, phase):
         drain(ref, recv_sem.at[phase], n - 1)
 
     def scatter_start(src, dst, phase):
         def send(i, carry):
-            peer = lax.rem(me + i, n)
+            peer = peer_of(i)
             pltpu.make_async_remote_copy(
                 src_ref=src.at[peer],
                 dst_ref=dst.at[me],
@@ -147,12 +173,12 @@
             ).start()
             return carry
 
-        lax.fori_loop(1, n, send, 0)
+        lax.fori_loop(0, n - 1, send, 0)
         dst[me] = src[me]
 
     def scatter_sum(dst, phase):
         drain(dst, recv_sem.at[phase], n - 1)
-        return jnp.sum(dst[...], axis=0)
+        return jnp.sum(dst[...].astype(F32), axis=0)
 
     def pack_rhs():
         tops = [
@@ -172,12 +198,14 @@
     def pack_terms(dst):
         for c in range(n // 2):
             cols = pl.ds(c * LANES, LANES)
+            first, second = [], []
             for a in range(2):
-                rows = pl.ds(8 * a, 8)
                 even = terms[pl.ds(16 * a, 8), cols]
                 odd = terms[pl.ds(16 * a + 8, 8), cols]
-                dst[2 * c, rows, :] = jnp.where(low, even, swap_halves(odd))
-                dst[2 * c + 1, rows, :] = jnp.where(low, swap_halves(even), odd)
+                first.append(jnp.where(low, even, swap_halves(odd)))
+                second.append(jnp.where(low, swap_halves(even), odd))
+            dst[2 * c] = jnp.concatenate(first, axis=0).astype(BF16)
+            dst[2 * c + 1] = jnp.concatenate(second, axis=0).astype(BF16)
 
     def columns(ref):
         return jnp.concatenate([ref[c] for c in range(n)], axis=1)
@@ -197,10 +225,13 @@
             total += jnp.where(where_at == first + q, table[8 * q : 8 * q + 8, :], 0.0)
         return total
 
+    loads[0].wait()
     packed_rhs = pack_rhs()
     pl.semaphore_wait(barrier, n - 1 + groups - 1)
     gather_start(g1, packed_rhs, 0)
 
+    for copy in loads[1:7]:
+        copy.wait()
     piece = leaf_rows.shape[1]
     at_list, low_list = [], []
     for s in range(4):
@@ -223,7 +254,7 @@
         lax.broadcasted_iota(jnp.int32, (LANES, LANES), 0) == (rows_p & (LANES - 1)), 1.0, 0.0
     ).astype(BF16)
 
-    loads[0].wait()
+    loads[7].wait()
     gather_wait(g1, 0)
     unpack(g1)
     full = dot_nt(xs[...], leaf_inv[...])
@@ -235,7 +266,7 @@
         axis=0,
     )
     gather_start(g2, ly.astype(BF16), 1)
-    loads[1].wait()
+    loads[8].wait()
     gather_wait(g2, 1)
     unpack(g2)
     updates = []
@@ -246,24 +277,17 @@
     spread(jnp.concatenate(updates, axis=1), leaf_at, 2 * n, height)
     acc = dot_nt(spread_hi[...], onehot[...]) + dot_nt(spread_lo[...], onehot[...])
     for q in range(2 * n):
-        s3[q % n, q // n] = acc[8 * q : 8 * q + 8, :]
-    width = root_rhs.shape[1]
-    per_slab = LANES // width
-    slab = lax.div(group * n + me, per_slab)
-    part = lax.rem(me, per_slab)
-    lane_part = lax.broadcasted_iota(jnp.int32, (8, LANES), 1) // width
-    mine = jnp.concatenate([root_rhs[...]] * per_slab, axis=1)
-    s3[slab, 1] = s3[slab, 1] - jnp.where(lane_part == part, mine, 0.0)
+        s3[q % n, q // n] = acc[8 * q : 8 * q + 8, :].astype(BF16)
     scatter_start(s3, r3, 2)
     sums = scatter_sum(r3, 2)
 
     prb = (parent_rhs[...] - sums[0]).astype(BF16)
     gather_start(g4, prb, 3)
-    loads[2].wait()
+    loads[9].wait()
     gather_wait(g4, 3)
     py = dot_nt(columns(g4), parent_inv[...])
     gather_start(g5, py.astype(BF16), 4)
-    loads[3].wait()
+    loads[10].wait()
     gather_wait(g5, 4)
     pupd = dot_nt(columns(g5), parent_panel[...])
     spread(pupd, parent_at, n, LANES)
@@ -272,6 +296,13 @@
     )
     for q in range(n):
         s6[q] = acc_p[8 * q : 8 * q + 8, :]
+    width = root_rhs.shape[1]
+    per_slab = LANES // width
+    slab = lax.div(group * n + me, per_slab)
+    part = lax.rem(me, per_slab)
+    lane_part = lax.broadcasted_iota(jnp.int32, (8, LANES), 1) // width
+    mine = jnp.concatenate([root_rhs[...]] * per_slab, axis=1)
+    s6[slab] = s6[slab] - jnp.where(lane_part == part, mine, 0.0)
     scatter_start(s6, r6, 5)
     partial = scatter_sum(r6, 5) + sums[1]
 
@@ -287,7 +318,7 @@
     drain(g7a, recv_sem.at[6], groups - 1)
     rrb = (-jnp.sum(g7a[...], axis=0)).astype(BF16)
     gather_start(g7b, rrb, 7)
-    loads[4].wait()
+    loads[11].wait()
     gather_wait(g7b, 7)
     ry = dot_nt(columns(g7b), root_inv[...])
     root_term = dot(ry.astype(BF16), root_inv[...])
@@ -368,14 +399,13 @@
         height = 4 * leaf_panel.shape[1]
         packed = (16, LANES)
         vmem = pl.BlockSpec(memory_space=pltpu.VMEM)
-        smem = pl.BlockSpec(memory_space=pltpu.SMEM)
         hbm = pl.BlockSpec(memory_space=pl.ANY)
         slabs = (n, 8, LANES)
         buffers = [
             ((n, *packed), BF16),
             ((n, *packed), BF16),
-            ((n, 2, 8, LANES), F32),
-            ((n, 2, 8, LANES), F32),
+            ((n, 2, 8, LANES), BF16),
+            ((n, 2, 8, LANES), BF16),
             (slabs, BF16),
             (slabs, BF16),
             (slabs, F32),
@@ -390,10 +420,10 @@
             (slabs, F32),
             (slabs, F32),
             (slabs, BF16),
-            ((n, *packed), F32),
-            ((n, *packed), F32),
-            ((n, *packed), F32),
-            ((n, *packed), F32),
+            ((n, *packed), BF16),
+            ((n, *packed), BF16),
+            ((n, *packed), BF16),
+            ((n, *packed), BF16),
         ]
         leaf_out, parent_out, root_out = pl.pallas_call(
             functools.partial(kernel, n, groups),
@@ -402,9 +432,16 @@
                 jax.ShapeDtypeStruct((8, LANES), F32),
                 jax.ShapeDtypeStruct(root_rhs.shape, F32),
             ),
-            in_specs=[vmem, vmem, vmem, vmem, smem, vmem, smem] + [hbm] * 5,
+            in_specs=[hbm] * 12,
             out_specs=(vmem, vmem, vmem),
             scratch_shapes=[
+                pltpu.VMEM(leaf_rhs.shape, F32),
+                pltpu.VMEM((8, LANES), F32),
+                pltpu.VMEM(root_rhs.shape, F32),
+                pltpu.VMEM(leaf_rows.shape, jnp.int32),
+                pltpu.SMEM(leaf_height.shape, jnp.int32),
+                pltpu.VMEM(parent_rows.shape, jnp.int32),
+                pltpu.SMEM(parent_height.shape, jnp.int32),
                 pltpu.VMEM((256, leaf_cols), BF16),
                 pltpu.VMEM((height, leaf_cols), BF16),
                 pltpu.VMEM((LANES, cols), BF16),
@@ -419,12 +456,12 @@
             ]
             + [pltpu.VMEM(shape, kind) for shape, kind in buffers]
             + [
-                pltpu.SemaphoreType.DMA((5,)),
+                pltpu.SemaphoreType.DMA((12,)),
                 pltpu.SemaphoreType.DMA((PHASES,)),
                 pltpu.SemaphoreType.DMA((PHASES,)),
             ],
             compiler_params=pltpu.CompilerParams(
-                collective_id=0, has_side_effects=True, vmem_limit_bytes=48 << 20
+                collective_id=0, has_side_effects=True, vmem_limit_bytes=67043328
             ),
             name="solve",
         )(

time: 106 us -> 94.4 us (0.89)
  local copies, waits for them, and re-layouts: 10.9 us -> 3.92 us
  Pallas kernels: 93.1 us -> 88.9 us
    unnamed x22 -> x2, local copies, waits for them, and re-layouts: 10.2 us -> 2.54 us
    pallas_call x1, Pallas kernels: 93.1 us -> 88.9 us  [shards(): pl.pallas_call(functools.partial(kernel, n, groups), out_shape=(jax.Shape...]
where the time goes in v2:
time: 94.4 us; the launch traced here: 94.1 us
  Pallas kernels  88.9 us (94%)
  local copies, waits for them, and re-layouts  3.92 us (4%)
  between operations  1.29 us (1%)
    pallas_call x1, Pallas kernels, shards(): pl.pallas_call(functools.partial(kernel, n, groups), out_shape=(jax.Shape...  88.9 us
    unnamed x2, local copies, waits for them, and re-layouts  2.54 us

profile of v2, /device:TPU:1, one launch (start us, length us, event | category | flops | bytes accessed | tf_op | source)
XLA Modules:
  0.0 94.1 jit_solution(17885874160826845177)
XLA Ops:
  1.3 88.9 %solve.1 = (f32[16,128]{1,0:T(8,128)}, f32[8,128]{1,0:T(8,128)}, f32[8,32]{1,0:T(8,128)}) custom-call(f32[8,4,64]{2,1,0:T(4,128)} %leaf_rhs_hbm.1, f32[8,128]{1,0:T(8,128)} %bitcast.16, f32[8,32]{1,0:T(8,128)} %root_rhs_hbm.1, s32[4,256]{1,0:T(4,128)} %leaf_rows_hbm.1, s32[4]{0:T(128)} %leaf_height_hbm.1, s32[1,128]{1,0:T(1,128)} %parent_rows_hbm.1, ...), custom_call_target="tpu_custom_call" | custom-call | tf_op jit(solution)/shard_map/solve/pallas_call | solution.py:428
  90.1 0.8 reshape.20
  90.9 0.6 copy.15
  91.5 1.3 %copy.20 = f32[8,1,128]{2,1,0:T(1,128)} copy(f32[8,1,128]{2,1,0:T(1,128)} %bitcast.17) | data formatting | bytes 8192
  92.8 1.3 %copy.21 = f32[8,32]{1,0:T(8,128)} copy(f32[8,32]{1,0:T(8,128)} %get-tuple-element.17) | data formatting | bytes 2048

commit v3 on v2

--- a/solution.py
+++ b/solution.py
@@ -12,7 +12,8 @@
 LANES = 128
 HALF = 64
 NT = (((1,), (1,)), ((), ()))
-PHASES = 15
+PHASES = 16
+BULK = 15
 
 
 def dot(a, b):
@@ -57,18 +58,21 @@
     parent_inv,
     parent_panel,
     root_inv,
+    panel_cols,
+    all_rows,
     onehot,
     onehot_p,
     xs,
-    spread_hi,
-    spread_lo,
+    spread_ref,
+    spread_p,
     terms,
     g1,
     g2,
-    s3,
-    r3,
+    s3p,
+    r3p,
+    s3r,
+    r3r,
     g4,
-    g5,
     s6,
     r6,
     g7a,
@@ -76,8 +80,6 @@
     s8,
     r8,
     g9,
-    s10,
-    r10,
     s11,
     r11,
     g12,
@@ -94,26 +96,30 @@
 
     barrier = pltpu.get_barrier_semaphore()
 
-    def peer_of(i):
+    if n == 32:
+        z, x, core = lax.div(me, 8), lax.rem(lax.div(me, 2), 4), lax.rem(me, 2)
+    order = [(x, c) for x in (2, 3, 1, 0) for c in (1, 0)]
+
+    def each_peer(act):
         if n != 32:
-            return lax.rem(me + i + 1, n)
-
-        def far_first(a):
-            high = lax.div(a, 2)
-            return 2 * (1 - high) + lax.rem(high + a, 2)
-
-        z = lax.rem(lax.div(me, 8) + far_first(lax.div(i, 8)), 4)
-        x = lax.rem(lax.div(me, 2) + far_first(lax.rem(lax.div(i, 2), 4)), 4)
-        return 8 * z + 2 * x + lax.rem(me + 1 - lax.rem(i, 2), 2)
-
-    def greet_row(i, carry):
-        pl.semaphore_signal(barrier, inc=1, device_id={"rows": peer_of(i)})
-        return carry
-
-    lax.fori_loop(0, n - 1, greet_row, 0)
+            lax.fori_loop(1, n, lambda i, carry: (act(lax.rem(me + i, n)), carry)[1], 0)
+            return
+
+        def ring(i, carry):
+            base = 8 * lax.rem(z + (2 + i) - 4 * lax.div(i, 2) + lax.div(i, 2), 4)
+            for dx, dc in order:
+                act(base + 2 * lax.rem(x + dx, 4) + lax.rem(core + dc, 2))
+            return carry
+
+        lax.fori_loop(0, 3, ring, 0)
+        for dx, dc in order[:-1]:
+            act(8 * z + 2 * lax.rem(x + dx, 4) + lax.rem(core + dc, 2))
+
+    each_peer(lambda peer: pl.semaphore_signal(barrier, inc=1, device_id={"rows": peer}))
     for i in range(1, groups):
         pl.semaphore_signal(barrier, inc=1, device_id={"leaf": lax.rem(group + i, groups)})
 
+    own_cols = parent_panel_hbm.at[:, pl.ds(pl.multiple_of(me * LANES, LANES), LANES)]
     loads = [
         pltpu.make_async_copy(src, dst, load_sem.at[i])
         for i, (src, dst) in enumerate(
@@ -130,6 +136,7 @@
                 (parent_inv_hbm, parent_inv),
                 (parent_panel_hbm, parent_panel),
                 (root_inv_hbm, root_inv),
+                (own_cols, panel_cols.at[me]),
             )
         )
     ]
@@ -145,36 +152,45 @@
 
     def gather_start(ref, value, phase):
         ref[me] = value
-
-        def send(i, carry):
-            pltpu.make_async_remote_copy(
+        each_peer(
+            lambda peer: pltpu.make_async_remote_copy(
                 src_ref=ref.at[me],
                 dst_ref=ref.at[me],
                 send_sem=send_sem.at[phase],
                 recv_sem=recv_sem.at[phase],
-                device_id={"rows": peer_of(i)},
+                device_id={"rows": peer},
             ).start()
-            return carry
-
-        lax.fori_loop(0, n - 1, send, 0)
+        )
 
     def gather_wait(ref, phase):
         drain(ref, recv_sem.at[phase], n - 1)
 
     def scatter_start(src, dst, phase):
-        def send(i, carry):
-            peer = peer_of(i)
-            pltpu.make_async_remote_copy(
+        each_peer(
+            lambda peer: pltpu.make_async_remote_copy(
                 src_ref=src.at[peer],
                 dst_ref=dst.at[me],
                 send_sem=send_sem.at[phase],
                 recv_sem=recv_sem.at[phase],
                 device_id={"rows": peer},
             ).start()
+        )
+        dst[me] = src[me]
+
+    def send_panel(first, last):
+        def send(i, carry):
+            peer = lax.rem(me + i, n)
+            cols = pl.ds(pl.multiple_of(peer * LANES, LANES), LANES)
+            pltpu.make_async_remote_copy(
+                src_ref=parent_panel.at[:, cols],
+                dst_ref=panel_cols.at[me],
+                send_sem=send_sem.at[BULK],
+                recv_sem=recv_sem.at[BULK],
+                device_id={"rows": peer},
+            ).start()
             return carry
 
-        lax.fori_loop(0, n - 1, send, 0)
-        dst[me] = src[me]
+        lax.fori_loop(first, last, send, 0)
 
     def scatter_sum(dst, phase):
         drain(dst, recv_sem.at[phase], n - 1)
@@ -210,14 +226,14 @@
     def columns(ref):
         return jnp.concatenate([ref[c] for c in range(n)], axis=1)
 
-    def spread(value, where_at, blocks, width):
-        high = value.astype(BF16).astype(F32)
-        rest = value - high
-        for q in range(0, blocks, 2):
-            rows = pl.ds(8 * q, 16)
-            for part, ref in ((high, spread_hi), (rest, spread_lo)):
-                pair = [jnp.where(where_at == q + k, part, 0.0) for k in range(2)]
-                ref[rows, 0:width] = jnp.concatenate(pair, axis=0).astype(BF16)
+    def spread(value, where_at, first, ref):
+        pair = jnp.concatenate([value, value], axis=0).astype(BF16)
+        second = lax.broadcasted_iota(jnp.int32, pair.shape, 0) >= 8
+        at = jnp.concatenate([where_at, where_at], axis=0) - jnp.where(second, 1, 0)
+        at = at.astype(F32).astype(BF16)
+        for q in range(0, n, 2):
+            number = jnp.array(first + q, BF16)
+            ref[pl.ds(8 * q, 16), :] = jnp.where(at == number, pair, jnp.array(0.0, BF16))
 
     def pick(table, where_at, first):
         total = jnp.zeros(where_at.shape, F32)
@@ -229,9 +245,22 @@
     packed_rhs = pack_rhs()
     pl.semaphore_wait(barrier, n - 1 + groups - 1)
     gather_start(g1, packed_rhs, 0)
-
     for copy in loads[1:7]:
         copy.wait()
+    all_rows[me] = parent_rows[...]
+    each_peer(
+        lambda peer: pltpu.make_async_remote_copy(
+            src_ref=all_rows.at[me],
+            dst_ref=all_rows.at[me],
+            send_sem=send_sem.at[4],
+            recv_sem=recv_sem.at[4],
+            device_id={"rows": peer},
+        ).start()
+    )
+    loads[10].wait()
+    quarter = -(-(n - 1) // 4)
+    send_panel(1, 1 + quarter)
+
     piece = leaf_rows.shape[1]
     at_list, low_list = [], []
     for s in range(4):
@@ -245,14 +274,6 @@
     onehot[...] = jnp.where(
         lax.broadcasted_iota(jnp.int32, (LANES, height), 0) == leaf_low, 1.0, 0.0
     ).astype(BF16)
-    rows_p = parent_rows[...]
-    pos_p = me * LANES + lax.broadcasted_iota(jnp.int32, (1, LANES), 1)
-    parent_at = jnp.broadcast_to(
-        jnp.where(pos_p < parent_height[0], rows_p >> 7, -1), (8, LANES)
-    )
-    onehot_p[...] = jnp.where(
-        lax.broadcasted_iota(jnp.int32, (LANES, LANES), 0) == (rows_p & (LANES - 1)), 1.0, 0.0
-    ).astype(BF16)
 
     loads[7].wait()
     gather_wait(g1, 0)
@@ -266,6 +287,18 @@
         axis=0,
     )
     gather_start(g2, ly.astype(BF16), 1)
+    send_panel(1 + quarter, 1 + 2 * quarter)
+
+    drain(all_rows, recv_sem.at[4], n - 1)
+    rows_p = jnp.concatenate([all_rows[c] for c in range(n)], axis=1)
+    pos_p = lax.broadcasted_iota(jnp.int32, rows_p.shape, 1)
+    parent_at = jnp.broadcast_to(
+        jnp.where(pos_p < parent_height[0], rows_p >> 7, -1), (8, n * LANES)
+    )
+    onehot_p[...] = jnp.where(
+        lax.broadcasted_iota(jnp.int32, onehot_p.shape, 0) == (rows_p & (LANES - 1)), 1.0, 0.0
+    ).astype(BF16)
+
     loads[8].wait()
     gather_wait(g2, 1)
     unpack(g2)
@@ -274,28 +307,27 @@
         a, b = s // 2, s % 2
         got = dot_nt(xs[16 * b : 16 * b + 16, :], leaf_panel[pl.ds(s * piece, piece), :])
         updates.append(got[8 * a : 8 * a + 8, :])
-    spread(jnp.concatenate(updates, axis=1), leaf_at, 2 * n, height)
-    acc = dot_nt(spread_hi[...], onehot[...]) + dot_nt(spread_lo[...], onehot[...])
-    for q in range(2 * n):
-        s3[q % n, q // n] = acc[8 * q : 8 * q + 8, :].astype(BF16)
-    scatter_start(s3, r3, 2)
-    sums = scatter_sum(r3, 2)
-
-    prb = (parent_rhs[...] - sums[0]).astype(BF16)
+    updates = jnp.concatenate(updates, axis=1)
+    spread(updates, leaf_at, 0, spread_ref)
+    s3p[...] = dot_nt(spread_ref[...], onehot[...]).astype(BF16).reshape(n, 8, LANES)
+    scatter_start(s3p, r3p, 2)
+    send_panel(1 + 2 * quarter, 1 + 3 * quarter)
+    spread(updates, leaf_at, n, spread_ref)
+    s3r[...] = dot_nt(spread_ref[...], onehot[...]).astype(BF16).reshape(n, 8, LANES)
+    pacc = scatter_sum(r3p, 2)
+
+    prb = (parent_rhs[...] - pacc).astype(BF16)
     gather_start(g4, prb, 3)
+    scatter_start(s3r, r3r, 10)
+    send_panel(1 + 3 * quarter, n)
     loads[9].wait()
+    loads[12].wait()
     gather_wait(g4, 3)
     py = dot_nt(columns(g4), parent_inv[...])
-    gather_start(g5, py.astype(BF16), 4)
-    loads[10].wait()
-    gather_wait(g5, 4)
-    pupd = dot_nt(columns(g5), parent_panel[...])
-    spread(pupd, parent_at, n, LANES)
-    acc_p = dot_nt(spread_hi[0 : 8 * n, 0:LANES], onehot_p[...]) + dot_nt(
-        spread_lo[0 : 8 * n, 0:LANES], onehot_p[...]
-    )
-    for q in range(n):
-        s6[q] = acc_p[8 * q : 8 * q + 8, :]
+    drain(panel_cols, recv_sem.at[BULK], n - 1)
+    cols_of = panel_cols[...].reshape(n * LANES, LANES)
+    spread(dot_nt(py.astype(BF16), cols_of), parent_at, 0, spread_p)
+    s6[...] = dot_nt(spread_p[...], onehot_p[...]).reshape(n, 8, LANES)
     width = root_rhs.shape[1]
     per_slab = LANES // width
     slab = lax.div(group * n + me, per_slab)
@@ -304,7 +336,8 @@
     mine = jnp.concatenate([root_rhs[...]] * per_slab, axis=1)
     s6[slab] = s6[slab] - jnp.where(lane_part == part, mine, 0.0)
     scatter_start(s6, r6, 5)
-    partial = scatter_sum(r6, 5) + sums[1]
+    racc = scatter_sum(r3r, 10)
+    partial = scatter_sum(r6, 5) + racc
 
     g7a[group] = partial
     for i in range(1, groups):
@@ -330,32 +363,39 @@
     gather_wait(g9, 9)
 
     rxb = g9[...].reshape(n * 8, LANES)
-    parent_anc = pick(dot(rxb, onehot_p[...]), parent_at, 0).astype(BF16)
-    parent_term = dot(parent_anc, parent_panel[...])
+    pt = jnp.zeros((8, LANES), F32)
+    chunk = 4 * LANES
+    for c in range(0, n * LANES, chunk):
+        cols = slice(c, c + chunk)
+        got = pick(dot(rxb, onehot_p[:, cols]), parent_at[:, cols], 0).astype(BF16)
+        pt += dot(got, panel_cols[c // LANES : (c + chunk) // LANES].reshape(chunk, LANES))
+    pvb = (py - pt).astype(BF16)
+    parent_term = dot(pvb, parent_inv[...])
     for c in range(n):
-        s10[c] = parent_term[:, c * LANES : (c + 1) * LANES]
-    scatter_start(s10, r10, 10)
-    leaf_anc = pick(dot(rxb, onehot[...]), leaf_at, n)
+        s11[c] = parent_term[:, c * LANES : (c + 1) * LANES]
+    scatter_start(s11, r11, 11)
+    root_anc = [
+        pick(
+            dot(rxb, onehot[:, s * piece : (s + 1) * piece]),
+            leaf_at[:, s * piece : (s + 1) * piece],
+            n,
+        )
+        for s in range(4)
+    ]
     mine = jnp.where(lane_part == part, g9[slab].astype(F32), 0.0)
     root_out[...] = functools.reduce(
         lambda x, y: x + y, [mine[:, k * width : (k + 1) * width] for k in range(per_slab)]
     )
-    pvb = (py - scatter_sum(r10, 10)).astype(BF16)
-    parent_term = dot(pvb, parent_inv[...])
-    for c in range(n):
-        s11[c] = parent_term[:, c * LANES : (c + 1) * LANES]
-    scatter_start(s11, r11, 11)
     parent_sol = scatter_sum(r11, 11)
+    gather_start(g12, parent_sol.astype(BF16), 12)
     parent_out[...] = parent_sol
-    gather_start(g12, parent_sol.astype(BF16), 12)
     gather_wait(g12, 12)
 
     pxb = g12[...].reshape(n * 8, LANES)
-    leaf_anc = (leaf_anc + pick(dot(pxb, onehot[...]), leaf_at, 0)).astype(BF16)
     for s in range(4):
-        terms[pl.ds(8 * s, 8), :] = dot(
-            leaf_anc[:, s * piece : (s + 1) * piece], leaf_panel[pl.ds(s * piece, piece), :]
-        )
+        cols = slice(s * piece, (s + 1) * piece)
+        got = (root_anc[s] + pick(dot(pxb, onehot[:, cols]), leaf_at[:, cols], 0)).astype(BF16)
+        terms[pl.ds(8 * s, 8), :] = dot(got, leaf_panel[pl.ds(s * piece, piece), :])
     pack_terms(s13)
     scatter_start(s13, r13, 13)
     lvb = ly - scatter_sum(r13, 13)
@@ -368,12 +408,26 @@
     terms[...] = dot(jnp.concatenate(blocks, axis=0).astype(BF16), leaf_inv[...])
     pack_terms(s14)
     scatter_start(s14, r14, 14)
-    leaf_out[...] = scatter_sum(r14, 14)
+    result = scatter_sum(r14, 14)
+    for a in range(2):
+        rows = result[8 * a : 8 * a + 8, :]
+        leaf_out[:, 2 * a, :] = rows[:, :HALF]
+        leaf_out[:, 2 * a + 1, :] = swap_halves(rows)[:, :HALF]
 
     for phase, ref in enumerate(
-        (g1, g2, r3, g4, g5, r6, g7a, g7b, r8, g9, r10, r11, g12, r13, r14)
+        (g1, g2, r3p, g4, all_rows, r6, g7a, g7b, r8, g9, r3r, r11, g12, r13, r14, panel_cols)
     ):
         drain(ref, send_sem.at[phase], (groups if phase == 6 else n) - 1)
+
+
+def store(count, *refs):
+    copies = [
+        pltpu.make_async_copy(refs[i], refs[count + i], refs[-1].at[i]) for i in range(count)
+    ]
+    for copy in copies:
+        copy.start()
+    for copy in copies:
+        copy.wait()
 
 
 def solution(mesh):
@@ -399,13 +453,14 @@
         height = 4 * leaf_panel.shape[1]
         packed = (16, LANES)
         vmem = pl.BlockSpec(memory_space=pltpu.VMEM)
-        hbm = pl.BlockSpec(memory_space=pl.ANY)
+        hbm = pl.BlockSpec(memory_space=pltpu.HBM)
         slabs = (n, 8, LANES)
         buffers = [
             ((n, *packed), BF16),
             ((n, *packed), BF16),
-            ((n, 2, 8, LANES), BF16),
-            ((n, 2, 8, LANES), BF16),
+            (slabs, BF16),
+            (slabs, BF16),
+            (slabs, BF16),
             (slabs, BF16),
             (slabs, BF16),
             (slabs, F32),
@@ -415,8 +470,6 @@
             (slabs, F32),
             (slabs, F32),
             (slabs, BF16),
-            (slabs, F32),
-            (slabs, F32),
             (slabs, F32),
             (slabs, F32),
             (slabs, BF16),
@@ -428,7 +481,7 @@
         leaf_out, parent_out, root_out = pl.pallas_call(
             functools.partial(kernel, n, groups),
             out_shape=(
-                jax.ShapeDtypeStruct(packed, F32),
+                jax.ShapeDtypeStruct((8, 4, HALF), F32),
                 jax.ShapeDtypeStruct((8, LANES), F32),
                 jax.ShapeDtypeStruct(root_rhs.shape, F32),
             ),
@@ -447,39 +500,54 @@
                 pltpu.VMEM((LANES, cols), BF16),
                 pltpu.VMEM((LANES, cols), BF16),
                 pltpu.VMEM((LANES, cols), BF16),
+                pltpu.VMEM((n, LANES, LANES), BF16),
+                pltpu.VMEM((n, 1, LANES), jnp.int32),
                 pltpu.VMEM((LANES, height), BF16),
-                pltpu.VMEM((LANES, LANES), BF16),
+                pltpu.VMEM((LANES, cols), BF16),
                 pltpu.VMEM((32, leaf_cols), BF16),
-                pltpu.VMEM((16 * n, height), BF16),
-                pltpu.VMEM((16 * n, height), BF16),
+                pltpu.VMEM((8 * n, height), BF16),
+                pltpu.VMEM((8 * n, cols), BF16),
                 pltpu.VMEM((32, leaf_cols), F32),
             ]
             + [pltpu.VMEM(shape, kind) for shape, kind in buffers]
             + [
-                pltpu.SemaphoreType.DMA((12,)),
+                pltpu.SemaphoreType.DMA((13,)),
                 pltpu.SemaphoreType.DMA((PHASES,)),
                 pltpu.SemaphoreType.DMA((PHASES,)),
             ],
             compiler_params=pltpu.CompilerParams(
-                collective_id=0, has_side_effects=True, vmem_limit_bytes=67043328
+                collective_id=0, has_side_effects=True, vmem_limit_bytes=48 << 20
             ),
             name="solve",
         )(
-            leaf_rhs,
-            parent_rhs[:, 0, :],
-            root_rhs,
-            leaf_rows,
-            leaf_height,
-            parent_rows,
-            parent_height,
-            leaf_inv.reshape(-1, leaf_cols),
-            leaf_panel.reshape(-1, leaf_cols),
-            parent_inv[0],
-            parent_panel[0],
-            root_inv,
+            *(
+                x if x.size == 1 else pltpu.with_memory_space_constraint(x, pltpu.HBM)
+                for x in (
+                    leaf_rhs,
+                    parent_rhs[:, 0, :],
+                    root_rhs,
+                    leaf_rows,
+                    leaf_height,
+                    parent_rows,
+                    parent_height,
+                    leaf_inv.reshape(-1, leaf_cols),
+                    leaf_panel.reshape(-1, leaf_cols),
+                    parent_inv[0],
+                    parent_panel[0],
+                    root_inv,
+                )
+            )
         )
-        leaf_sol = leaf_out.reshape(2, 8, 2, HALF).transpose(1, 0, 2, 3).reshape(8, 4, HALF)
-        return leaf_sol, parent_out[:, None, :], root_out
+        results = (leaf_out, parent_out, root_out)
+        leaf_out, parent_out, root_out = pl.pallas_call(
+            functools.partial(store, 3),
+            out_shape=tuple(jax.ShapeDtypeStruct(r.shape, r.dtype) for r in results),
+            in_specs=[vmem] * 3,
+            out_specs=(hbm,) * 3,
+            scratch_shapes=[pltpu.SemaphoreType.DMA((3,))],
+            name="store",
+        )(*(pltpu.with_memory_space_constraint(r, pltpu.VMEM) for r in results))
+        return leaf_out, parent_out[:, None, :], root_out
 
     return jax.shard_map(
         shards,

time: 94.4 us -> 88.7 us (0.940)
  local copies, waits for them, and re-layouts: 3.92 us -> 0 us
  Pallas kernels: 88.9 us -> 87.2 us
    unnamed x2 -> x0, local copies, waits for them, and re-layouts: 2.54 us -> none
    pallas_call x1, Pallas kernels: 88.9 us -> 86.6 us  [shards(): pl.pallas_call(functools.partial(kernel, n, groups), out_shape=(jax.Shape...]
where the time goes in v3:
time: 88.7 us; the launch traced here: 88.5 us
  Pallas kernels  87.2 us (98%)
  between operations  1.29 us (1%)
    pallas_call x1, Pallas kernels, shards(): pl.pallas_call(functools.partial(kernel, n, groups), out_shape=(jax.Shape...  86.6 us

profile of v3, /device:TPU:1, one launch (start us, length us, event | category | flops | bytes accessed | tf_op | source)
XLA Modules:
  0.0 88.5 jit_solution(3639360297620592009)
XLA Ops:
  1.3 86.6 %solve.1 = (f32[8,4,64]{2,1,0:T(4,128)S(1)}, f32[8,128]{1,0:T(8,128)S(1)}, f32[8,32]{1,0:T(8,128)S(1)}) custom-call(f32[8,4,64]{2,1,0:T(4,128)} %leaf_rhs_hbm.1, f32[8,128]{1,0:T(8,128)} %bitcast.12, f32[8,32]{1,0:T(8,128)} %root_rhs_hbm.1, s32[4,256]{1,0:T(4,128)} %leaf_rows_hbm.1, s32[4]{0:T(128)} %leaf_height_hbm.1, s32[1,128]{1,0:T(1,128)} %parent_rows_hbm.1, ...), custom_call_target="tpu_custom_call" | custom-call | tf_op jit(solution)/shard_map/solve/pallas_call | solution.py:481
  87.9 0.6 store.1

commit v4 on v3

--- a/solution.py
+++ b/solution.py
@@ -11,6 +11,7 @@
 BF16 = jnp.bfloat16
 LANES = 128
 HALF = 64
+WIDE = 256
 NT = (((1,), (1,)), ((), ()))
 PHASES = 16
 BULK = 15
@@ -63,8 +64,7 @@
     onehot,
     onehot_p,
     xs,
-    spread_ref,
-    spread_p,
+    panel_root,
     terms,
     g1,
     g2,
@@ -134,7 +134,6 @@
                 (leaf_inv_hbm, leaf_inv),
                 (leaf_panel_hbm, leaf_panel),
                 (parent_inv_hbm, parent_inv),
-                (parent_panel_hbm, parent_panel),
                 (root_inv_hbm, root_inv),
                 (own_cols, panel_cols.at[me]),
             )
@@ -142,6 +141,15 @@
     ]
     for copy in loads:
         copy.start()
+
+    def load_cols(c, carry):
+        cols = pl.ds(pl.multiple_of(c * LANES, LANES), LANES)
+        pltpu.make_async_copy(
+            parent_panel_hbm.at[:, cols], parent_panel.at[c], load_sem.at[12]
+        ).start()
+        return carry
+
+    lax.fori_loop(0, n, load_cols, 0)
 
     low = lax.broadcasted_iota(jnp.int32, (8, LANES), 1) < HALF
     low16 = lax.broadcasted_iota(jnp.int32, (16, LANES), 1) < HALF
@@ -177,12 +185,17 @@
         )
         dst[me] = src[me]
 
-    def send_panel(first, last):
+    def send_panel(turn):
         def send(i, carry):
-            peer = lax.rem(me + i, n)
-            cols = pl.ds(pl.multiple_of(peer * LANES, LANES), LANES)
+            if n == 32:
+                dz, dc = lax.div(i, 2), lax.rem(i, 2)
+                dx = lax.rem(turn + 4 - dz, 4)
+                row = 8 * lax.rem(z + dz, 4) + 2 * lax.rem(x + dx, 4)
+                peer = row + lax.rem(core + dc, 2)
+            else:
+                peer = lax.rem(me + turn * n // 4 + i, n)
             pltpu.make_async_remote_copy(
-                src_ref=parent_panel.at[:, cols],
+                src_ref=parent_panel.at[peer],
                 dst_ref=panel_cols.at[me],
                 send_sem=send_sem.at[BULK],
                 recv_sem=recv_sem.at[BULK],
@@ -190,7 +203,7 @@
             ).start()
             return carry
 
-        lax.fori_loop(first, last, send, 0)
+        lax.fori_loop(0 if turn else 1, n // 4, send, 0)
 
     def scatter_sum(dst, phase):
         drain(dst, recv_sem.at[phase], n - 1)
@@ -226,20 +239,49 @@
     def columns(ref):
         return jnp.concatenate([ref[c] for c in range(n)], axis=1)
 
-    def spread(value, where_at, first, ref):
+    blocks = n // 2
+
+    def spread(value, where_at, first):
         pair = jnp.concatenate([value, value], axis=0).astype(BF16)
         second = lax.broadcasted_iota(jnp.int32, pair.shape, 0) >= 8
         at = jnp.concatenate([where_at, where_at], axis=0) - jnp.where(second, 1, 0)
         at = at.astype(F32).astype(BF16)
-        for q in range(0, n, 2):
-            number = jnp.array(first + q, BF16)
-            ref[pl.ds(8 * q, 16), :] = jnp.where(at == number, pair, jnp.array(0.0, BF16))
+        return jnp.concatenate(
+            [
+                jnp.where(at == jnp.array(first + q, BF16), pair, jnp.array(0.0, BF16))
+                for q in range(0, blocks, 2)
+            ],
+            axis=0,
+        )
+
+    def put_blocks(dst, acc):
+        for c in range(n):
+            part = acc[8 * (c // 2) : 8 * (c // 2) + 8, LANES * (c % 2) : LANES * (c % 2 + 1)]
+            dst[c] = part.astype(dst.dtype)
+
+    def get_blocks(ref):
+        return jnp.concatenate(
+            [jnp.concatenate([ref[2 * q], ref[2 * q + 1]], axis=1) for q in range(blocks)], axis=0
+        )
 
     def pick(table, where_at, first):
         total = jnp.zeros(where_at.shape, F32)
-        for q in range(n):
+        for q in range(blocks):
             total += jnp.where(where_at == first + q, table[8 * q : 8 * q + 8, :], 0.0)
         return total
+
+    def root_order(first, last):
+        at = jnp.broadcast_to(parent_at[0:1, :], (16, n * LANES)).astype(F32).astype(BF16)
+        for q in range(first, last):
+            mine = at == jnp.array(q, BF16)
+            chosen = jnp.concatenate(
+                [
+                    jnp.where(mine, onehot_p[16 * i : 16 * i + 16, :], jnp.array(0.0, BF16))
+                    for i in range(WIDE // 16)
+                ],
+                axis=0,
+            )
+            panel_root[pl.ds(q * WIDE, WIDE), :] = dot(chosen, cols_of).astype(BF16)
 
     loads[0].wait()
     packed_rhs = pack_rhs()
@@ -257,22 +299,21 @@
             device_id={"rows": peer},
         ).start()
     )
-    loads[10].wait()
-    quarter = -(-(n - 1) // 4)
-    send_panel(1, 1 + quarter)
+    pltpu.make_async_copy(parent_panel, parent_panel, load_sem.at[12]).wait()
+    send_panel(2)
 
     piece = leaf_rows.shape[1]
     at_list, low_list = [], []
     for s in range(4):
         rows_s = leaf_rows[s : s + 1, :]
         pos = me * piece + lax.broadcasted_iota(jnp.int32, (1, piece), 1)
-        at_list.append(jnp.where(pos < leaf_height[s], rows_s >> 7, -1))
-        low_list.append(rows_s & (LANES - 1))
+        at_list.append(jnp.where(pos < leaf_height[s], rows_s >> 8, -1))
+        low_list.append(rows_s & (WIDE - 1))
     height = 4 * piece
     leaf_at = jnp.broadcast_to(jnp.concatenate(at_list, axis=1), (8, height))
     leaf_low = jnp.concatenate(low_list, axis=1)
     onehot[...] = jnp.where(
-        lax.broadcasted_iota(jnp.int32, (LANES, height), 0) == leaf_low, 1.0, 0.0
+        lax.broadcasted_iota(jnp.int32, (WIDE, height), 0) == leaf_low, 1.0, 0.0
     ).astype(BF16)
 
     loads[7].wait()
@@ -287,47 +328,57 @@
         axis=0,
     )
     gather_start(g2, ly.astype(BF16), 1)
-    send_panel(1 + quarter, 1 + 2 * quarter)
+    send_panel(1)
 
     drain(all_rows, recv_sem.at[4], n - 1)
     rows_p = jnp.concatenate([all_rows[c] for c in range(n)], axis=1)
     pos_p = lax.broadcasted_iota(jnp.int32, rows_p.shape, 1)
     parent_at = jnp.broadcast_to(
-        jnp.where(pos_p < parent_height[0], rows_p >> 7, -1), (8, n * LANES)
+        jnp.where(pos_p < parent_height[0], rows_p >> 8, -1), (8, n * LANES)
     )
     onehot_p[...] = jnp.where(
-        lax.broadcasted_iota(jnp.int32, onehot_p.shape, 0) == (rows_p & (LANES - 1)), 1.0, 0.0
+        lax.broadcasted_iota(jnp.int32, onehot_p.shape, 0) == (rows_p & (WIDE - 1)), 1.0, 0.0
     ).astype(BF16)
 
     loads[8].wait()
     gather_wait(g2, 1)
     unpack(g2)
     updates = []
+    acc = jnp.zeros((8 * blocks, WIDE), F32)
     for s in range(4):
         a, b = s // 2, s % 2
-        got = dot_nt(xs[16 * b : 16 * b + 16, :], leaf_panel[pl.ds(s * piece, piece), :])
+        cols = slice(s * piece, (s + 1) * piece)
+        got = dot_nt(xs[16 * b : 16 * b + 16, :], leaf_panel[cols, :])
         updates.append(got[8 * a : 8 * a + 8, :])
-    updates = jnp.concatenate(updates, axis=1)
-    spread(updates, leaf_at, 0, spread_ref)
-    s3p[...] = dot_nt(spread_ref[...], onehot[...]).astype(BF16).reshape(n, 8, LANES)
+        acc += dot_nt(spread(updates[s], leaf_at[:, cols], 0), onehot[:, cols])
+    put_blocks(s3p, acc)
     scatter_start(s3p, r3p, 2)
-    send_panel(1 + 2 * quarter, 1 + 3 * quarter)
-    spread(updates, leaf_at, n, spread_ref)
-    s3r[...] = dot_nt(spread_ref[...], onehot[...]).astype(BF16).reshape(n, 8, LANES)
+    send_panel(3)
+    acc = jnp.zeros((8 * blocks, WIDE), F32)
+    for s in range(4):
+        cols = slice(s * piece, (s + 1) * piece)
+        acc += dot_nt(spread(updates[s], leaf_at[:, cols], blocks), onehot[:, cols])
+    put_blocks(s3r, acc)
     pacc = scatter_sum(r3p, 2)
 
     prb = (parent_rhs[...] - pacc).astype(BF16)
     gather_start(g4, prb, 3)
     scatter_start(s3r, r3r, 10)
-    send_panel(1 + 3 * quarter, n)
+    send_panel(0)
     loads[9].wait()
-    loads[12].wait()
+    loads[11].wait()
     gather_wait(g4, 3)
     py = dot_nt(columns(g4), parent_inv[...])
     drain(panel_cols, recv_sem.at[BULK], n - 1)
     cols_of = panel_cols[...].reshape(n * LANES, LANES)
-    spread(dot_nt(py.astype(BF16), cols_of), parent_at, 0, spread_p)
-    s6[...] = dot_nt(spread_p[...], onehot_p[...]).reshape(n, 8, LANES)
+    pyb = py.astype(BF16)
+    acc = jnp.zeros((8 * blocks, WIDE), F32)
+    chunk = 4 * LANES
+    for c in range(0, n * LANES, chunk):
+        cols = slice(c, c + chunk)
+        got = dot_nt(pyb, cols_of[cols, :])
+        acc += dot_nt(spread(got, parent_at[:, cols], 0), onehot_p[:, cols])
+    put_blocks(s6, acc)
     width = root_rhs.shape[1]
     per_slab = LANES // width
     slab = lax.div(group * n + me, per_slab)
@@ -336,6 +387,7 @@
     mine = jnp.concatenate([root_rhs[...]] * per_slab, axis=1)
     s6[slab] = s6[slab] - jnp.where(lane_part == part, mine, 0.0)
     scatter_start(s6, r6, 5)
+    root_order(0, (2 * blocks) // 8)
     racc = scatter_sum(r3r, 10)
     partial = scatter_sum(r6, 5) + racc
 
@@ -348,37 +400,36 @@
             recv_sem=recv_sem.at[6],
             device_id={"leaf": lax.rem(group + i, groups)},
         ).start()
+    root_order((2 * blocks) // 8, (3 * blocks) // 8)
     drain(g7a, recv_sem.at[6], groups - 1)
     rrb = (-jnp.sum(g7a[...], axis=0)).astype(BF16)
     gather_start(g7b, rrb, 7)
-    loads[11].wait()
+    root_order((3 * blocks) // 8, (5 * blocks) // 8)
+    loads[10].wait()
     gather_wait(g7b, 7)
     ry = dot_nt(columns(g7b), root_inv[...])
     root_term = dot(ry.astype(BF16), root_inv[...])
     for c in range(n):
         s8[c] = root_term[:, c * LANES : (c + 1) * LANES]
     scatter_start(s8, r8, 8)
+    root_order((5 * blocks) // 8, (7 * blocks) // 8)
     root_slab = scatter_sum(r8, 8)
     gather_start(g9, root_slab.astype(BF16), 9)
+    root_order((7 * blocks) // 8, blocks)
     gather_wait(g9, 9)
 
-    rxb = g9[...].reshape(n * 8, LANES)
-    pt = jnp.zeros((8, LANES), F32)
-    chunk = 4 * LANES
-    for c in range(0, n * LANES, chunk):
-        cols = slice(c, c + chunk)
-        got = pick(dot(rxb, onehot_p[:, cols]), parent_at[:, cols], 0).astype(BF16)
-        pt += dot(got, panel_cols[c // LANES : (c + chunk) // LANES].reshape(chunk, LANES))
+    pt = dot(columns(g9), panel_root[...])
     pvb = (py - pt).astype(BF16)
     parent_term = dot(pvb, parent_inv[...])
     for c in range(n):
         s11[c] = parent_term[:, c * LANES : (c + 1) * LANES]
     scatter_start(s11, r11, 11)
+    rxb = get_blocks(g9)
     root_anc = [
         pick(
             dot(rxb, onehot[:, s * piece : (s + 1) * piece]),
             leaf_at[:, s * piece : (s + 1) * piece],
-            n,
+            blocks,
         )
         for s in range(4)
     ]
@@ -391,7 +442,7 @@
     parent_out[...] = parent_sol
     gather_wait(g12, 12)
 
-    pxb = g12[...].reshape(n * 8, LANES)
+    pxb = get_blocks(g12)
     for s in range(4):
         cols = slice(s * piece, (s + 1) * piece)
         got = (root_anc[s] + pick(dot(pxb, onehot[:, cols]), leaf_at[:, cols], 0)).astype(BF16)
@@ -400,12 +451,12 @@
     scatter_start(s13, r13, 13)
     lvb = ly - scatter_sum(r13, 13)
     none = jnp.zeros((8, LANES), F32)
-    blocks = []
+    rows_of = []
     for s in range(4):
         a, b = s // 2, s % 2
         held = jnp.where(low if b == 0 else ~low, lvb[8 * a : 8 * a + 8, :], 0.0)
-        blocks.append(jnp.concatenate([held, none] if a == 0 else [none, held], axis=1))
-    terms[...] = dot(jnp.concatenate(blocks, axis=0).astype(BF16), leaf_inv[...])
+        rows_of.append(jnp.concatenate([held, none] if a == 0 else [none, held], axis=1))
+    terms[...] = dot(jnp.concatenate(rows_of, axis=0).astype(BF16), leaf_inv[...])
     pack_terms(s14)
     scatter_start(s14, r14, 14)
     result = scatter_sum(r14, 14)
@@ -498,15 +549,14 @@
                 pltpu.VMEM((256, leaf_cols), BF16),
                 pltpu.VMEM((height, leaf_cols), BF16),
                 pltpu.VMEM((LANES, cols), BF16),
-                pltpu.VMEM((LANES, cols), BF16),
+                pltpu.VMEM((n, LANES, LANES), BF16),
                 pltpu.VMEM((LANES, cols), BF16),
                 pltpu.VMEM((n, LANES, LANES), BF16),
                 pltpu.VMEM((n, 1, LANES), jnp.int32),
-                pltpu.VMEM((LANES, height), BF16),
-                pltpu.VMEM((LANES, cols), BF16),
+                pltpu.VMEM((WIDE, height), BF16),
+                pltpu.VMEM((WIDE, cols), BF16),
                 pltpu.VMEM((32, leaf_cols), BF16),
-                pltpu.VMEM((8 * n, height), BF16),
-                pltpu.VMEM((8 * n, cols), BF16),
+                pltpu.VMEM((cols, LANES), BF16),
                 pltpu.VMEM((32, leaf_cols), F32),
             ]
             + [pltpu.VMEM(shape, kind) for shape, kind in buffers]

time: 88.7 us -> 83.1 us (0.937)
  Pallas kernels: 87.2 us -> 81.5 us
    pallas_call x1, Pallas kernels: 86.6 us -> 80.8 us  [shards(): pl.pallas_call(functools.partial(kernel, n, groups), out_shape=(jax.Shape...]
where the time goes in v4:
time: 83.1 us; the launch traced here: 82.9 us
  Pallas kernels  81.5 us (98%)
  between operations  1.45 us (2%)
    pallas_call x1, Pallas kernels, shards(): pl.pallas_call(functools.partial(kernel, n, groups), out_shape=(jax.Shape...  80.8 us

profile of v4, /device:TPU:1, one launch (start us, length us, event | category | flops | bytes accessed | tf_op | source)
XLA Modules:
  0.0 82.9 jit_solution(16040097461392226889)
XLA Ops:
  1.3 80.8 %solve.1 = (f32[8,4,64]{2,1,0:T(4,128)S(1)}, f32[8,128]{1,0:T(8,128)S(1)}, f32[8,32]{1,0:T(8,128)S(1)}) custom-call(f32[8,4,64]{2,1,0:T(4,128)} %leaf_rhs_hbm.1, f32[8,128]{1,0:T(8,128)} %bitcast.12, f32[8,32]{1,0:T(8,128)} %root_rhs_hbm.1, s32[4,256]{1,0:T(4,128)} %leaf_rows_hbm.1, s32[4]{0:T(128)} %leaf_height_hbm.1, s32[1,128]{1,0:T(1,128)} %parent_rows_hbm.1, ...), custom_call_target="tpu_custom_call" | custom-call | tf_op jit(solution)/shard_map/solve/pallas_call | solution.py:532
  82.1 0.6 store.1

commit v5 on v4

--- a/solution.py
+++ b/solution.py
@@ -385,7 +385,7 @@
     part = lax.rem(me, per_slab)
     lane_part = lax.broadcasted_iota(jnp.int32, (8, LANES), 1) // width
     mine = jnp.concatenate([root_rhs[...]] * per_slab, axis=1)
-    s6[slab] = s6[slab] - jnp.where(lane_part == part, mine, 0.0)
+    s6[slab] = (s6[slab].astype(F32) - jnp.where(lane_part == part, mine, 0.0)).astype(BF16)
     scatter_start(s6, r6, 5)
     root_order(0, (2 * blocks) // 8)
     racc = scatter_sum(r3r, 10)
@@ -410,7 +410,7 @@
     ry = dot_nt(columns(g7b), root_inv[...])
     root_term = dot(ry.astype(BF16), root_inv[...])
     for c in range(n):
-        s8[c] = root_term[:, c * LANES : (c + 1) * LANES]
+        s8[c] = root_term[:, c * LANES : (c + 1) * LANES].astype(BF16)
     scatter_start(s8, r8, 8)
     root_order((5 * blocks) // 8, (7 * blocks) // 8)
     root_slab = scatter_sum(r8, 8)
@@ -422,7 +422,7 @@
     pvb = (py - pt).astype(BF16)
     parent_term = dot(pvb, parent_inv[...])
     for c in range(n):
-        s11[c] = parent_term[:, c * LANES : (c + 1) * LANES]
+        s11[c] = parent_term[:, c * LANES : (c + 1) * LANES].astype(BF16)
     scatter_start(s11, r11, 11)
     rxb = get_blocks(g9)
     root_anc = [
@@ -514,15 +514,15 @@
             (slabs, BF16),
             (slabs, BF16),
             (slabs, BF16),
-            (slabs, F32),
-            (slabs, F32),
+            (slabs, BF16),
+            (slabs, BF16),
             ((groups, 8, LANES), F32),
             (slabs, BF16),
-            (slabs, F32),
-            (slabs, F32),
-            (slabs, BF16),
-            (slabs, F32),
-            (slabs, F32),
+            (slabs, BF16),
+            (slabs, BF16),
+            (slabs, BF16),
+            (slabs, BF16),
+            (slabs, BF16),
             (slabs, BF16),
             ((n, *packed), BF16),
             ((n, *packed), BF16),

time: 83.1 us -> 82.6 us (level)
  no operation moved by 1% of the time
where the time goes in v5:
time: 82.6 us; the launch traced here: 82.4 us
  Pallas kernels  80.9 us (98%)
  between operations  1.45 us (2%)
    pallas_call x1, Pallas kernels, shards(): pl.pallas_call(functools.partial(kernel, n, groups), out_shape=(jax.Shape...  80.3 us

profile of v5, /device:TPU:1, one launch (start us, length us, event | category | flops | bytes accessed | tf_op | source)
XLA Modules:
  0.0 82.4 jit_solution(475442086608318083)
XLA Ops:
  1.3 80.3 %solve.1 = (f32[8,4,64]{2,1,0:T(4,128)S(1)}, f32[8,128]{1,0:T(8,128)S(1)}, f32[8,32]{1,0:T(8,128)S(1)}) custom-call(f32[8,4,64]{2,1,0:T(4,128)} %leaf_rhs_hbm.1, f32[8,128]{1,0:T(8,128)} %bitcast.12, f32[8,32]{1,0:T(8,128)} %root_rhs_hbm.1, s32[4,256]{1,0:T(4,128)} %leaf_rows_hbm.1, s32[4]{0:T(128)} %leaf_height_hbm.1, s32[1,128]{1,0:T(1,128)} %parent_rows_hbm.1, ...), custom_call_target="tpu_custom_call" | custom-call | tf_op jit(solution)/shard_map/solve/pallas_call | solution.py:532
  81.6 0.6 store.1

commit v6 on v5

--- a/solution.py
+++ b/solution.py
@@ -186,14 +186,17 @@
         dst[me] = src[me]
 
     def send_panel(turn):
-        def send(i, carry):
-            if n == 32:
-                dz, dc = lax.div(i, 2), lax.rem(i, 2)
-                dx = lax.rem(turn + 4 - dz, 4)
-                row = 8 * lax.rem(z + dz, 4) + 2 * lax.rem(x + dx, 4)
-                peer = row + lax.rem(core + dc, 2)
-            else:
-                peer = lax.rem(me + turn * n // 4 + i, n)
+        if n == 32:
+            extra = {2: (2, 2), 1: (1, 3), 3: (3, 1)}[turn]
+            steps = [(dz, (turn - dz) % 4) for dz in range(4)] + [extra]
+            moves = [(dz, dx, dc) for dz, dx in steps for dc in range(2)]
+            peers = [
+                8 * lax.rem(z + dz, 4) + 2 * lax.rem(x + dx, 4) + lax.rem(core + dc, 2)
+                for dz, dx, dc in moves + ([(0, 0, 1)] if turn == 2 else [])
+            ]
+        else:
+            peers = [lax.rem(me + i, n) for i in range(turn, n, 3)]
+        for peer in peers:
             pltpu.make_async_remote_copy(
                 src_ref=parent_panel.at[peer],
                 dst_ref=panel_cols.at[me],
@@ -201,9 +204,6 @@
                 recv_sem=recv_sem.at[BULK],
                 device_id={"rows": peer},
             ).start()
-            return carry
-
-        lax.fori_loop(0 if turn else 1, n // 4, send, 0)
 
     def scatter_sum(dst, phase):
         drain(dst, recv_sem.at[phase], n - 1)
@@ -364,7 +364,6 @@
     prb = (parent_rhs[...] - pacc).astype(BF16)
     gather_start(g4, prb, 3)
     scatter_start(s3r, r3r, 10)
-    send_panel(0)
     loads[9].wait()
     loads[11].wait()
     gather_wait(g4, 3)

time: 82.6 us -> 81.3 us (0.984)
  Pallas kernels: 80.9 us -> 79.6 us
    pallas_call x1, Pallas kernels: 80.3 us -> 79 us  [shards(): pl.pallas_call(functools.partial(kernel, n, groups), out_shape=(jax.Shape...]
where the time goes in v6:
time: 81.3 us; the launch traced here: 81.1 us
  Pallas kernels  79.6 us (98%)
  between operations  1.45 us (2%)
    pallas_call x1, Pallas kernels, shards(): pl.pallas_call(functools.partial(kernel, n, groups), out_shape=(jax.Shape...  79 us

profile of v6, /device:TPU:1, one launch (start us, length us, event | category | flops | bytes accessed | tf_op | source)
XLA Modules:
  0.0 81.1 jit_solution(12590080839122911497)
XLA Ops:
  1.3 79.0 %solve.1 = (f32[8,4,64]{2,1,0:T(4,128)S(1)}, f32[8,128]{1,0:T(8,128)S(1)}, f32[8,32]{1,0:T(8,128)S(1)}) custom-call(f32[8,4,64]{2,1,0:T(4,128)} %leaf_rhs_hbm.1, f32[8,128]{1,0:T(8,128)} %bitcast.12, f32[8,32]{1,0:T(8,128)} %root_rhs_hbm.1, s32[4,256]{1,0:T(4,128)} %leaf_rows_hbm.1, s32[4]{0:T(128)} %leaf_height_hbm.1, s32[1,128]{1,0:T(1,128)} %parent_rows_hbm.1, ...), custom_call_target="tpu_custom_call" | custom-call | tf_op jit(solution)/shard_map/solve/pallas_call | solution.py:531
  80.3 0.6 store.1
